TPU v7x, 256 devices: a whole 4x4x8 slice. The times are simulated.
256 devices in a mesh: space: 32 (over z, y), member: 8 (over x, core).
Axes of the slice: x: 4, y: 4, z: 8, core: 2. Of those that a mesh axis runs over, the one named last changes fastest.
Arguments:
- increment: bfloat16 [3072, 64, 128], P('space', 'member'), may hold values from -6 to 6
- interp: bfloat16 [3072, 128, 128], P('space'), may hold values from -0.25 to 0.25
- owner: int32 [3072, 1], P('space'), may hold values from 0 to 31; in each aligned block of 96 rows (0 to 95, 96 to 191, ...) at most 6 rows name the same one
- local_block: int32 [3072], P('space'), may hold values from 0 to 23
- ensemble: bfloat16 [80, 768, 64, 128], P('member', 'space'), may hold values from -6 to 6
- modes: float32 [64, 4], replicated, may hold values from -2 to 2
Outputs:
- applied_fine: float32 [3072, 64, 128], P('space', 'member')
Inputs may be any that keep to these rules, and one draw needn't show every extreme that they name: `owner`: among the rows of one device no value appears more than 6 times, and some value appears exactly 6 times.
All inputs are finite; a program needn't handle non-finite values.
Results may differ from a plain program's by a relative error of at most 0.0038.
Values may be sent and summed in bfloat16 or wider, within the bound.
A program may use at most 64 MiB of HBM per device.

v0:
```python
import jax
import jax.numpy as jnp
from jax import lax
from jax.sharding import PartitionSpec as P


def sent_together(arrays, axis, split_dim, concat_dim, along):
    columns = [a.reshape(*a.shape[:along], -1) for a in arrays]
    both = jnp.concatenate(columns, axis=along)
    result, at, gathered = (
        lax.all_to_all(both, axis, split_axis=split_dim, concat_axis=concat_dim, tiled=True),
        0,
        [],
    )
    for a, column in zip(arrays, columns):
        section = result[..., at : at + column.shape[along]]
        gathered.append(section.reshape(*section.shape[:along], *a.shape[along:]))
        at += column.shape[along]
    return tuple(gathered)


def from_everyone(array, axis):
    count = lax.axis_size(axis)
    return lax.all_to_all(
        jnp.broadcast_to(array[None], (count, *array.shape)), axis, 0, 0, tiled=True
    )


def in_order(parts, dim):
    lengths = list(parts.shape[1:])
    lengths[dim] *= parts.shape[0]
    return jnp.moveaxis(parts, 0, dim).reshape(lengths)


def gather_directly(array, axis, dim):
    parts = from_everyone(array, axis)
    return in_order(parts, dim)


def in_blocks(array, dim, count):
    before, after = (array.shape[:dim], array.shape[dim + 1 :])
    return jnp.moveaxis(array.reshape(*before, count, -1, *after), dim, 0)


def summed_on_arrival(array, axis, dim):
    count = lax.axis_size(axis)
    parts = lax.all_to_all(in_blocks(array, dim, count), axis, 0, 0, tiled=True)
    return jnp.sum(parts, axis=0)


def on_device(increment, interp, owner, local_block, ensemble, modes):
    highest = lax.Precision.HIGHEST
    fine_count, levels_here, width = increment.shape
    coarse_count = ensemble.shape[1]
    owners = lax.axis_size("space")
    groups = lax.axis_size("member")
    member_count = ensemble.shape[0]
    pieces = jnp.einsum("bli,bij->blj", increment, interp, preferred_element_type=jnp.float32)
    pieces_flat = pieces.reshape(fine_count, levels_here * width)
    target_owner = owner[:, 0]
    capacity = max(2, 2 * ((fine_count + owners - 1) // owners))
    matches = (target_owner[:, None] == jnp.arange(owners, dtype=jnp.int32)[None, :]).astype(
        jnp.int32
    )
    slot_rank = jnp.sum((jnp.cumsum(matches, axis=0) - matches) * matches, axis=1)
    slot_index = target_owner * capacity + slot_rank
    placing = (
        jnp.arange(owners * capacity, dtype=jnp.int32)[:, None] == slot_index[None, :]
    ).astype(jnp.float32)
    send_values = jnp.dot(
        placing, pieces_flat, precision=highest, preferred_element_type=jnp.float32
    )
    send_index = jnp.dot(
        placing,
        (local_block + 1).astype(jnp.float32),
        precision=highest,
        preferred_element_type=jnp.float32,
    )
    recv_values, recv_index = sent_together((send_values, send_index), "space", 0, 0, 1)
    collect = (
        jnp.arange(coarse_count, dtype=jnp.float32)[:, None] + 1.0 == recv_index[None, :]
    ).astype(jnp.float32)
    restricted_part = jnp.dot(
        collect, recv_values, precision=highest, preferred_element_type=jnp.float32
    )
    restricted_half = restricted_part.astype(jnp.bfloat16).reshape(coarse_count, levels_here, width)
    restricted = gather_directly(restricted_half, "member", 1)
    restricted_wide = restricted.astype(jnp.float32)

    def member_step(total, member):
        values = member.astype(jnp.float32)
        schur = values * restricted_wide
        coefficients = jnp.einsum("clj,lk->ckj", schur, modes, precision=highest)
        rebuilt = jnp.einsum("ckj,lk->clj", coefficients, modes, precision=highest)
        return (total + values * rebuilt, None)

    start_total = jnp.zeros(restricted.shape, jnp.float32)
    total = lax.scan(member_step, start_total, ensemble)[0]
    total = total / (member_count * groups - 1)
    summed = summed_on_arrival(total, "member", 1)
    applied = summed.astype(jnp.bfloat16).reshape(coarse_count, levels_here * width)
    reply = jnp.dot(
        collect.T.astype(jnp.bfloat16), applied, preferred_element_type=jnp.float32
    ).astype(jnp.bfloat16)
    back_values = lax.all_to_all(reply, "space", split_axis=0, concat_axis=0, tiled=True)
    fine_values = jnp.dot(
        placing.T.astype(jnp.bfloat16), back_values, preferred_element_type=jnp.float32
    ).astype(jnp.bfloat16)
    fine_values = fine_values.reshape(fine_count, levels_here, width)
    return jnp.einsum("blj,bij->bli", fine_values, interp, preferred_element_type=jnp.float32)


def solution(mesh):
    in_specs = (
        P("space", "member", None),
        P("space", None, None),
        P("space", None),
        P("space"),
        P("member", "space", None, None),
        P(),
    )
    out_specs = P("space", "member", None)
    return jax.shard_map(
        on_device, mesh=mesh, in_specs=in_specs, out_specs=out_specs, check_vma=False
    )
```

profile of v0, /device:TPU:1, one launch (start us, length us, event | category | flops | bytes accessed | tf_op | source)
XLA Modules:
  0.0 166.2 jit_solution(674743978308671963)
XLA Ops:
  0.0 0.0 copy-start
  0.0 0.0 copy-start.2
  0.0 0.9 fusion.20
  0.9 0.1 reduce_window_sum.11
  1.0 0.8 select_reduce_fusion
  1.9 0.7 multiply_add_fusion.1
  2.5 0.0 copy-done
  2.6 1.8 %fusion.28 = f32[96,8,128]{2,1,0:T(8,128)S(1)} fusion(bf16[96,8,128]{2,1,0:T(8,128)(2,1)} %param.8, bf16[96,128,128]{2,1,0:T(8,128)(2,1)S(1)} %copy-done), kind=kOutput, calls=%fused_computation.48 | convolution fusion | flops 25165824 | bytes 3735552 | tf_op jit(solution)/shard_map/bli,bij->blj/dot_general | solution.py:58
  4.4 0.8 reshape.64
  5.2 0.0 copy-done.2
  5.2 0.1 fusion.12
  5.4 0.2 concatenate.6
  5.5 0.4 copy.11
  5.9 1.5 fusion.10
  7.4 0.1 pad_maximum_fusion
  7.5 1.6 copy.12
  9.1 12.1 %all-to-all-start = ((f32[32,6,1025]{2,1,0:T(8,128)}), f32[32,6,1025]{2,1,0:T(8,128)}, u32[]{:S(2)}, u32[]{:S(2)}) async-start(f32[32,6,1025]{2,1,0:T(8,128)} %copy.12), calls=%async_computation | async-start | bytes 2359296 | tf_op jit(solution)/shard_map/all_to_all | solution.py:11
  21.2 0.0 copy-start.1
  21.3 28.6 %all-to-all-done = f32[32,6,1025]{2,1,0:T(8,128)} async-done(((f32[32,6,1025]{2,1,0:T(8,128)}), f32[32,6,1025]{2,1,0:T(8,128)}, u32[]{:S(2)}, u32[]{:S(2)}) %all-to-all-start) | async-done | bytes 787232 | tf_op jit(solution)/shard_map/all_to_all | solution.py:11
  49.9 2.4 %all_to_all.21 = f32[192,1025]{1,0:T(8,128)} reshape(f32[32,6,1025]{2,1,0:T(8,128)} %all-to-all-done) | data formatting | bytes 1574400 | tf_op jit(solution)/shard_map/all_to_all | solution.py:11
  52.2 1.0 slice_reduce_fusion
  53.2 1.5 fusion.8
  54.8 0.8 broadcast_in_dim.16
  55.6 7.4 %all-to-all-start.1 = ((bf16[8,24,8,128]{3,2,1,0:T(8,128)(2,1)}), bf16[8,24,8,128]{3,2,1,0:T(8,128)(2,1)S(1)}, u32[]{:S(2)}, u32[]{:S(2)}) async-start(bf16[8,24,8,128]{3,2,1,0:T(8,128)(2,1)} %broadcast_in_dim.16), calls=%async_computation.1 | async-start | bytes 786432 | tf_op jit(solution)/shard_map/all_to_all | solution.py:24
  63.0 8.1 %all-to-all-done.1 = bf16[8,24,8,128]{3,2,1,0:T(8,128)(2,1)S(1)} async-done(((bf16[8,24,8,128]{3,2,1,0:T(8,128)(2,1)}), bf16[8,24,8,128]{3,2,1,0:T(8,128)(2,1)S(1)}, u32[]{:S(2)}, u32[]{:S(2)}) %all-to-all-start.1) | async-done | bytes 393248 | tf_op jit(solution)/shard_map/all_to_all | solution.py:24
  71.1 1.0 convert_bitcast_fusion
  72.0 0.0 copy-done.1
  72.0 48.2 %while.11 = (s32[]{:T(128)}, f32[24,64,128]{2,1,0:T(8,128)}, bf16[10,24,64,128]{3,2,1,0:T(8,128)(2,1)}, f32[24,64,128]{2,1,0:T(8,128)}, f32[64,4]{0,1:T(4,128)S(1)}, /*index=5*/s32[]{:T(128)}, s32[]{:T(128)}) while((s32[]{:T(128)}, f32[24,64,128]{2,1,0:T(8,128)}, bf16[10,24,64,128]{3,2,1,0:T(8,128)(2,1)}, ...), condition=%wide.region_3.4_spmd.clone, body=%wide.region_2.3_spmd.clone.sunk | while | flops 20054020 | bytes 3246683 | solution.py:98
  72.0 1.8 %convolution_bitcast_fusion.3 = f32[24,4,128]{2,1,0:T(4,128)S(1)} fusion(f32[24,64,128]{2,1,0:T(8,128)} %get-tuple-element.109, bf16[10,24,64,128]{3,2,1,0:T(8,128)(2,1)} %get-tuple-element.108, s32[]{:T(128)} %get-tuple-element.99, f32[64,4]{0,1:T(4,128)S(1)} %get-tuple-element.110), kind=kOutput, calls=%fused_computation.3.clone.1 | convolution fusion | flops 9830400 | bytes 1230336 | tf_op jit(solution)/shard_map/while/body/eval_jaxpr/clj,lk->ckj/dot_general | solution.py:93
  73.8 2.8 %fusion.44 = f32[24,64,128]{2,1,0:T(8,128)} fusion(f32[24,4,128]{2,1,0:T(4,128)S(1)} %convolution_bitcast_fusion.3, f32[24,64,128]{2,1,0:T(8,128)} %get-tuple-element.100, pred[]{:T(512)S(6)} %compare.3, bf16[10,24,64,128]{3,2,1,0:T(8,128)(2,1)} %get-tuple-element.108, s32[]{:T(128)} %get-tuple-element.99, f32[64,4]{0,1:T(4,128)S(1)} %get-tuple-element.110), kind=kOutput, calls=%fused_computation.2.clone.1 | convolution fusion | flops 10223616 | bytes 2016261 | tf_op jit(solution)/shard_map/while/body/eval_jaxpr/ckj,lk->clj/dot_general | solution.py:94
  76.7 1.8 %convolution_bitcast_fusion.3 = f32[24,4,128]{2,1,0:T(4,128)S(1)} fusion(f32[24,64,128]{2,1,0:T(8,128)} %get-tuple-element.109, bf16[10,24,64,128]{3,2,1,0:T(8,128)(2,1)} %get-tuple-element.108, s32[]{:T(128)} %get-tuple-element.99, f32[64,4]{0,1:T(4,128)S(1)} %get-tuple-element.110), kind=kOutput, calls=%fused_computation.3.clone.1 | convolution fusion | flops 9830400 | bytes 1230336 | tf_op jit(solution)/shard_map/while/body/eval_jaxpr/clj,lk->ckj/dot_general | solution.py:93
  78.5 3.0 %fusion.44 = f32[24,64,128]{2,1,0:T(8,128)} fusion(f32[24,4,128]{2,1,0:T(4,128)S(1)} %convolution_bitcast_fusion.3, f32[24,64,128]{2,1,0:T(8,128)} %get-tuple-element.100, pred[]{:T(512)S(6)} %compare.3, bf16[10,24,64,128]{3,2,1,0:T(8,128)(2,1)} %get-tuple-element.108, s32[]{:T(128)} %get-tuple-element.99, f32[64,4]{0,1:T(4,128)S(1)} %get-tuple-element.110), kind=kOutput, calls=%fused_computation.2.clone.1 | convolution fusion | flops 10223616 | bytes 2016261 | tf_op jit(solution)/shard_map/while/body/eval_jaxpr/ckj,lk->clj/dot_general | solution.py:94
  81.5 1.8 %convolution_bitcast_fusion.3 = f32[24,4,128]{2,1,0:T(4,128)S(1)} fusion(f32[24,64,128]{2,1,0:T(8,128)} %get-tuple-element.109, bf16[10,24,64,128]{3,2,1,0:T(8,128)(2,1)} %get-tuple-element.108, s32[]{:T(128)} %get-tuple-element.99, f32[64,4]{0,1:T(4,128)S(1)} %get-tuple-element.110), kind=kOutput, calls=%fused_computation.3.clone.1 | convolution fusion | flops 9830400 | bytes 1230336 | tf_op jit(solution)/shard_map/while/body/eval_jaxpr/clj,lk->ckj/dot_general | solution.py:93
  83.3 3.0 %fusion.44 = f32[24,64,128]{2,1,0:T(8,128)} fusion(f32[24,4,128]{2,1,0:T(4,128)S(1)} %convolution_bitcast_fusion.3, f32[24,64,128]{2,1,0:T(8,128)} %get-tuple-element.100, pred[]{:T(512)S(6)} %compare.3, bf16[10,24,64,128]{3,2,1,0:T(8,128)(2,1)} %get-tuple-element.108, s32[]{:T(128)} %get-tuple-element.99, f32[64,4]{0,1:T(4,128)S(1)} %get-tuple-element.110), kind=kOutput, calls=%fused_computation.2.clone.1 | convolution fusion | flops 10223616 | bytes 2016261 | tf_op jit(solution)/shard_map/while/body/eval_jaxpr/ckj,lk->clj/dot_general | solution.py:94
  86.3 1.8 %convolution_bitcast_fusion.3 = f32[24,4,128]{2,1,0:T(4,128)S(1)} fusion(f32[24,64,128]{2,1,0:T(8,128)} %get-tuple-element.109, bf16[10,24,64,128]{3,2,1,0:T(8,128)(2,1)} %get-tuple-element.108, s32[]{:T(128)} %get-tuple-element.99, f32[64,4]{0,1:T(4,128)S(1)} %get-tuple-element.110), kind=kOutput, calls=%fused_computation.3.clone.1 | convolution fusion | flops 9830400 | bytes 1230336 | tf_op jit(solution)/shard_map/while/body/eval_jaxpr/clj,lk->ckj/dot_general | solution.py:93
  88.1 3.0 %fusion.44 = f32[24,64,128]{2,1,0:T(8,128)} fusion(f32[24,4,128]{2,1,0:T(4,128)S(1)} %convolution_bitcast_fusion.3, f32[24,64,128]{2,1,0:T(8,128)} %get-tuple-element.100, pred[]{:T(512)S(6)} %compare.3, bf16[10,24,64,128]{3,2,1,0:T(8,128)(2,1)} %get-tuple-element.108, s32[]{:T(128)} %get-tuple-element.99, f32[64,4]{0,1:T(4,128)S(1)} %get-tuple-element.110), kind=kOutput, calls=%fused_computation.2.clone.1 | convolution fusion | flops 10223616 | bytes 2016261 | tf_op jit(solution)/shard_map/while/body/eval_jaxpr/ckj,lk->clj/dot_general | solution.py:94
  91.2 1.8 %convolution_bitcast_fusion.3 = f32[24,4,128]{2,1,0:T(4,128)S(1)} fusion(f32[24,64,128]{2,1,0:T(8,128)} %get-tuple-element.109, bf16[10,24,64,128]{3,2,1,0:T(8,128)(2,1)} %get-tuple-element.108, s32[]{:T(128)} %get-tuple-element.99, f32[64,4]{0,1:T(4,128)S(1)} %get-tuple-element.110), kind=kOutput, calls=%fused_computation.3.clone.1 | convolution fusion | flops 9830400 | bytes 1230336 | tf_op jit(solution)/shard_map/while/body/eval_jaxpr/clj,lk->ckj/dot_general | solution.py:93
  93.0 3.0 %fusion.44 = f32[24,64,128]{2,1,0:T(8,128)} fusion(f32[24,4,128]{2,1,0:T(4,128)S(1)} %convolution_bitcast_fusion.3, f32[24,64,128]{2,1,0:T(8,128)} %get-tuple-element.100, pred[]{:T(512)S(6)} %compare.3, bf16[10,24,64,128]{3,2,1,0:T(8,128)(2,1)} %get-tuple-element.108, s32[]{:T(128)} %get-tuple-element.99, f32[64,4]{0,1:T(4,128)S(1)} %get-tuple-element.110), kind=kOutput, calls=%fused_computation.2.clone.1 | convolution fusion | flops 10223616 | bytes 2016261 | tf_op jit(solution)/shard_map/while/body/eval_jaxpr/ckj,lk->clj/dot_general | solution.py:94
  96.0 1.8 %convolution_bitcast_fusion.3 = f32[24,4,128]{2,1,0:T(4,128)S(1)} fusion(f32[24,64,128]{2,1,0:T(8,128)} %get-tuple-element.109, bf16[10,24,64,128]{3,2,1,0:T(8,128)(2,1)} %get-tuple-element.108, s32[]{:T(128)} %get-tuple-element.99, f32[64,4]{0,1:T(4,128)S(1)} %get-tuple-element.110), kind=kOutput, calls=%fused_computation.3.clone.1 | convolution fusion | flops 9830400 | bytes 1230336 | tf_op jit(solution)/shard_map/while/body/eval_jaxpr/clj,lk->ckj/dot_general | solution.py:93
  97.8 3.0 %fusion.44 = f32[24,64,128]{2,1,0:T(8,128)} fusion(f32[24,4,128]{2,1,0:T(4,128)S(1)} %convolution_bitcast_fusion.3, f32[24,64,128]{2,1,0:T(8,128)} %get-tuple-element.100, pred[]{:T(512)S(6)} %compare.3, bf16[10,24,64,128]{3,2,1,0:T(8,128)(2,1)} %get-tuple-element.108, s32[]{:T(128)} %get-tuple-element.99, f32[64,4]{0,1:T(4,128)S(1)} %get-tuple-element.110), kind=kOutput, calls=%fused_computation.2.clone.1 | convolution fusion | flops 10223616 | bytes 2016261 | tf_op jit(solution)/shard_map/while/body/eval_jaxpr/ckj,lk->clj/dot_general | solution.py:94
  100.9 1.8 %convolution_bitcast_fusion.3 = f32[24,4,128]{2,1,0:T(4,128)S(1)} fusion(f32[24,64,128]{2,1,0:T(8,128)} %get-tuple-element.109, bf16[10,24,64,128]{3,2,1,0:T(8,128)(2,1)} %get-tuple-element.108, s32[]{:T(128)} %get-tuple-element.99, f32[64,4]{0,1:T(4,128)S(1)} %get-tuple-element.110), kind=kOutput, calls=%fused_computation.3.clone.1 | convolution fusion | flops 9830400 | bytes 1230336 | tf_op jit(solution)/shard_map/while/body/eval_jaxpr/clj,lk->ckj/dot_general | solution.py:93
  102.7 3.0 %fusion.44 = f32[24,64,128]{2,1,0:T(8,128)} fusion(f32[24,4,128]{2,1,0:T(4,128)S(1)} %convolution_bitcast_fusion.3, f32[24,64,128]{2,1,0:T(8,128)} %get-tuple-element.100, pred[]{:T(512)S(6)} %compare.3, bf16[10,24,64,128]{3,2,1,0:T(8,128)(2,1)} %get-tuple-element.108, s32[]{:T(128)} %get-tuple-element.99, f32[64,4]{0,1:T(4,128)S(1)} %get-tuple-element.110), kind=kOutput, calls=%fused_computation.2.clone.1 | convolution fusion | flops 10223616 | bytes 2016261 | tf_op jit(solution)/shard_map/while/body/eval_jaxpr/ckj,lk->clj/dot_general | solution.py:94
  105.7 1.8 %convolution_bitcast_fusion.3 = f32[24,4,128]{2,1,0:T(4,128)S(1)} fusion(f32[24,64,128]{2,1,0:T(8,128)} %get-tuple-element.109, bf16[10,24,64,128]{3,2,1,0:T(8,128)(2,1)} %get-tuple-element.108, s32[]{:T(128)} %get-tuple-element.99, f32[64,4]{0,1:T(4,128)S(1)} %get-tuple-element.110), kind=kOutput, calls=%fused_computation.3.clone.1 | convolution fusion | flops 9830400 | bytes 1230336 | tf_op jit(solution)/shard_map/while/body/eval_jaxpr/clj,lk->ckj/dot_general | solution.py:93
  107.5 3.0 %fusion.44 = f32[24,64,128]{2,1,0:T(8,128)} fusion(f32[24,4,128]{2,1,0:T(4,128)S(1)} %convolution_bitcast_fusion.3, f32[24,64,128]{2,1,0:T(8,128)} %get-tuple-element.100, pred[]{:T(512)S(6)} %compare.3, bf16[10,24,64,128]{3,2,1,0:T(8,128)(2,1)} %get-tuple-element.108, s32[]{:T(128)} %get-tuple-element.99, f32[64,4]{0,1:T(4,128)S(1)} %get-tuple-element.110), kind=kOutput, calls=%fused_computation.2.clone.1 | convolution fusion | flops 10223616 | bytes 2016261 | tf_op jit(solution)/shard_map/while/body/eval_jaxpr/ckj,lk->clj/dot_general | solution.py:94
  110.5 1.8 %convolution_bitcast_fusion.3 = f32[24,4,128]{2,1,0:T(4,128)S(1)} fusion(f32[24,64,128]{2,1,0:T(8,128)} %get-tuple-element.109, bf16[10,24,64,128]{3,2,1,0:T(8,128)(2,1)} %get-tuple-element.108, s32[]{:T(128)} %get-tuple-element.99, f32[64,4]{0,1:T(4,128)S(1)} %get-tuple-element.110), kind=kOutput, calls=%fused_computation.3.clone.1 | convolution fusion | flops 9830400 | bytes 1230336 | tf_op jit(solution)/shard_map/while/body/eval_jaxpr/clj,lk->ckj/dot_general | solution.py:93
  112.3 3.0 %fusion.44 = f32[24,64,128]{2,1,0:T(8,128)} fusion(f32[24,4,128]{2,1,0:T(4,128)S(1)} %convolution_bitcast_fusion.3, f32[24,64,128]{2,1,0:T(8,128)} %get-tuple-element.100, pred[]{:T(512)S(6)} %compare.3, bf16[10,24,64,128]{3,2,1,0:T(8,128)(2,1)} %get-tuple-element.108, s32[]{:T(128)} %get-tuple-element.99, f32[64,4]{0,1:T(4,128)S(1)} %get-tuple-element.110), kind=kOutput, calls=%fused_computation.2.clone.1 | convolution fusion | flops 10223616 | bytes 2016261 | tf_op jit(solution)/shard_map/while/body/eval_jaxpr/ckj,lk->clj/dot_general | solution.py:94
  115.4 1.8 %convolution_bitcast_fusion.3 = f32[24,4,128]{2,1,0:T(4,128)S(1)} fusion(f32[24,64,128]{2,1,0:T(8,128)} %get-tuple-element.109, bf16[10,24,64,128]{3,2,1,0:T(8,128)(2,1)} %get-tuple-element.108, s32[]{:T(128)} %get-tuple-element.99, f32[64,4]{0,1:T(4,128)S(1)} %get-tuple-element.110), kind=kOutput, calls=%fused_computation.3.clone.1 | convolution fusion | flops 9830400 | bytes 1230336 | tf_op jit(solution)/shard_map/while/body/eval_jaxpr/clj,lk->ckj/dot_general | solution.py:93
  117.2 3.0 %fusion.44 = f32[24,64,128]{2,1,0:T(8,128)} fusion(f32[24,4,128]{2,1,0:T(4,128)S(1)} %convolution_bitcast_fusion.3, f32[24,64,128]{2,1,0:T(8,128)} %get-tuple-element.100, pred[]{:T(512)S(6)} %compare.3, bf16[10,24,64,128]{3,2,1,0:T(8,128)(2,1)} %get-tuple-element.108, s32[]{:T(128)} %get-tuple-element.99, f32[64,4]{0,1:T(4,128)S(1)} %get-tuple-element.110), kind=kOutput, calls=%fused_computation.2.clone.1 | convolution fusion | flops 10223616 | bytes 2016261 | tf_op jit(solution)/shard_map/while/body/eval_jaxpr/ckj,lk->clj/dot_general | solution.py:94
  120.2 1.2 multiply_bitcast_fusion
  121.4 0.1 copy.14
  121.5 16.2 %all_to_all.31 = f32[8,24,8,128]{3,2,1,0:T(8,128)} all-to-all(f32[8,24,8,128]{3,2,1,0:T(8,128)S(1)} %copy.14), channel_id=1, replica_groups=mesh['space'=32,'member'=8] {'member'}, dimensions={0} | all-to-all | bytes 1572864 | tf_op jit(solution)/shard_map/all_to_all | solution.py:47
  137.7 1.8 %reduce_sum.19 = bf16[24,8,128]{2,1,0:T(8,128)(2,1)} reduce(f32[8,24,8,128]{3,2,1,0:T(8,128)} %all_to_all.31, f32[]{:T(128)} %constant.24.clone.1), dimensions={0}, to_apply=%region_4.5 | reduce | flops 172032 | bytes 835588 | tf_op jit(solution)/shard_map/reduce_sum | solution.py:48
  139.5 1.1 convolution_convert_fusion
  140.6 0.9 all_to_all.24
  141.5 20.8 %all_to_all.32 = bf16[32,6,1024]{2,1,0:T(8,128)(2,1)} all-to-all(bf16[32,6,1024]{2,1,0:T(8,128)(2,1)} %all_to_all.24), channel_id=1, replica_groups=mesh['space'=32,'member'=8] {'space'}, dimensions={0} | all-to-all | bytes 786432 | tf_op jit(solution)/shard_map/all_to_all | solution.py:105
  162.2 1.2 all_to_all.26
  163.4 0.2 fusion.7
  163.7 2.5 %fusion.29 = f32[96,8,128]{2,1,0:T(8,128)} fusion(bf16[96,8,128]{2,1,0:T(8,128)(2,1)S(1)} %bitcast.65, bf16[96,128,128]{2,1,0:T(8,128)(2,1)S(1)} %copy-done), kind=kOutput, calls=%fused_computation.49 | convolution fusion | flops 25165824 | bytes 3735552 | tf_op jit(solution)/shard_map/blj,bij->bli/dot_general | solution.py:110
  (5 shorter events, 0.1 us)
Async XLA Ops:
  0.0 2.5 %copy-start = (bf16[96,128,128]{2,1,0:T(8,128)(2,1)S(1)}, bf16[96,128,128]{2,1,0:T(8,128)(2,1)}, u32[]{:S(2)}) copy-start(bf16[96,128,128]{2,1,0:T(8,128)(2,1)} %param.9) | copy-start | bytes 9437188
  0.0 5.2 %copy-start.2 = (s32[96]{0:T(128)S(1)}, s32[96]{0:T(128)}, u32[]{:S(2)}) copy-start(s32[96]{0:T(128)} %param.11) | copy-start | bytes 1156
  9.1 40.8 %all-to-all-start = ((f32[32,6,1025]{2,1,0:T(8,128)}), f32[32,6,1025]{2,1,0:T(8,128)}, u32[]{:S(2)}, u32[]{:S(2)}) async-start(f32[32,6,1025]{2,1,0:T(8,128)} %copy.12), calls=%async_computation | async-start | bytes 2359296 | tf_op jit(solution)/shard_map/all_to_all | solution.py:11
  21.2 50.8 %copy-start.1 = (f32[64,4]{0,1:T(4,128)S(1)}, f32[64,4]{0,1:T(4,128)}, u32[]{:S(2)}) copy-start(f32[64,4]{0,1:T(4,128)} %param.13) | copy-start | bytes 3076
  55.6 15.5 %all-to-all-start.1 = ((bf16[8,24,8,128]{3,2,1,0:T(8,128)(2,1)}), bf16[8,24,8,128]{3,2,1,0:T(8,128)(2,1)S(1)}, u32[]{:S(2)}, u32[]{:S(2)}) async-start(bf16[8,24,8,128]{3,2,1,0:T(8,128)(2,1)} %broadcast_in_dim.16), calls=%async_computation.1 | async-start | bytes 786432 | tf_op jit(solution)/shard_map/all_to_all | solution.py:24
where the time goes:
time: 169 us; the launch traced here: 166 us
  matrix products  56.9 us (34%)
  blocking collectives  36.9 us (22%)
  waiting for transfers between devices  36.7 us (22%)
  starting transfers between devices  19.6 us (12%)
  local copies, waits for them, and re-layouts  9.32 us (6%)
  other arithmetic  6.58 us (4%)
    dot_general x10, matrix products, member_step(): rebuilt = jnp.einsum('ckj,lk->clj', coefficients, modes, precision=highest)  30.2 us
    all_to_all x1, waiting for transfers between devices, sent_together(): lax.all_to_all(both, axis, split_axis=split_dim, concat_axis=concat_dim,...  28.6 us
    all_to_all x1, blocking collectives, on_device(): lax.all_to_all(reply, 'space', split_axis=0, concat_axis=0, tiled=True)  20.8 us
    dot_general x10, matrix products, member_step(): coefficients = jnp.einsum('clj,lk->ckj', schur, modes, precision=highest)  17.9 us
    all_to_all x1, blocking collectives, summed_on_arrival(): parts = lax.all_to_all(in_blocks(array, dim, count), axis, 0, 0, tiled=True)  16.2 us
    all_to_all x1, starting transfers between devices, sent_together(): lax.all_to_all(both, axis, split_axis=split_dim, concat_axis=concat_dim,...  12.1 us
    all_to_all x1, waiting for transfers between devices, from_everyone(): lax.all_to_all(jnp.broadcast_to(array[None], (count, *array.shape)), axis...  8.08 us
    all_to_all x1, starting transfers between devices, from_everyone(): lax.all_to_all(jnp.broadcast_to(array[None], (count, *array.shape)), axis...  7.43 us
  transfers between devices with their start and end apart: 2, of which 2 were waited for; matrix products, arithmetic and copies ran while one was open for 0% of the time, Pallas kernels for 0%

commit v1 on v0

v1 whole, which is shorter than its diff:
```python
import functools
import jax
import jax.numpy as jnp
from jax import lax
from jax.experimental import pallas as pl
from jax.experimental.pallas import tpu as pltpu
from jax.sharding import PartitionSpec as P

MESH = pl.DeviceIdType.MESH
CAP = 6
F32 = jnp.float32
BF16 = jnp.bfloat16


def iota(shape, dim):
    return lax.broadcasted_iota(jnp.int32, shape, dim)


def dot(a, b):
    return jnp.dot(a, b, preferred_element_type=F32)


def one_hot(condition):
    return jnp.where(condition, 1.0, 0.0).astype(BF16)


def kernel(
    dims,
    interp_hbm,
    inc_hbm,
    ens_hbm,
    owner_ref,
    local_ref,
    modes_ref,
    out_ref,
    interp,
    inc,
    ens,
    pieces,
    send,
    recv,
    idx_send,
    idx_recv,
    unplace,
    collect,
    spread,
    levels_buf,
    contrib,
    arrived,
    reply,
    back,
    fine,
    load_sem,
    send_sem,
    recv_sem,
):
    n_space, n_member, fine_count, lev, members, coarse, width, chunks, scale = dims
    rows = CAP * lev
    slots = n_space * rows
    fine_rows = fine_count * lev
    coarse_rows = coarse * lev
    me = lax.axis_index("space")
    group = lax.axis_index("member")
    per = fine_count // chunks

    inc_copy = pltpu.make_async_copy(inc_hbm, inc, load_sem.at[chunks])
    inc_copy.start()
    loads = []
    for t in range(chunks):
        part = pl.ds(t * per, per)
        copy = pltpu.make_async_copy(interp_hbm.at[part], interp.at[part], load_sem.at[t])
        copy.start()
        loads.append(copy)
    ens_copy = pltpu.make_async_copy(ens_hbm, ens, load_sem.at[chunks + 1])
    ens_copy.start()

    barrier = pltpu.get_barrier_semaphore()

    def greet_space(k, carry):
        peer = {"space": lax.rem(me + k, n_space)}
        pl.semaphore_signal(barrier, inc=1, device_id=peer, device_id_type=MESH)
        return carry

    def greet_member(k, carry):
        peer = {"member": lax.rem(group + k, n_member)}
        pl.semaphore_signal(barrier, inc=1, device_id=peer, device_id_type=MESH)
        return carry

    lax.fori_loop(1, n_space, greet_space, 0)
    lax.fori_loop(1, n_member, greet_member, 0)

    owner_col = owner_ref[...].astype(F32)
    own_b = jnp.broadcast_to(owner_col, (fine_count, fine_count))
    down, across = iota((fine_count, fine_count), 0), iota((fine_count, fine_count), 1)
    owner_row = jnp.sum(jnp.where(down == across, own_b, 0.0), axis=0, keepdims=True)
    same = own_b == owner_row
    rank_row = jnp.sum(jnp.where(same & (down < across), 1.0, 0.0), axis=0, keepdims=True)
    rank_col = jnp.sum(jnp.where(same & (across < down), 1.0, 0.0), axis=1, keepdims=True)
    slot_row = owner_row * CAP + rank_row
    slot_col = owner_col * CAP + rank_col

    local_row = local_ref[...].astype(F32) + 1.0
    by_owner = jnp.where(
        iota((n_space, fine_count), 0).astype(F32) == owner_row, local_row, 0.0
    ).astype(BF16)
    by_rank = one_hot(iota((fine_count, 128), 1).astype(F32) == rank_col)
    table = dot(by_owner, by_rank)
    for d in range(n_space):
        idx_send[d] = table[d : d + 1, :]

    widen = one_hot(iota((fine_count, fine_rows), 1) // lev == iota((fine_count, fine_rows), 0))
    place_row = dot(jnp.broadcast_to(slot_row, (8, fine_count)).astype(BF16), widen)[0:1]
    place_row = place_row * lev + (iota((1, fine_rows), 1) % lev).astype(F32)

    inc_copy.wait()
    for t in range(chunks):
        loads[t].wait()

        @pl.loop(0, per // 2, unroll=4)
        def _(i):
            b = t * per + i * 2
            first = dot(inc[b], interp[b])
            second = dot(inc[b + 1], interp[b + 1])
            both = jnp.concatenate([first, second], axis=0).astype(BF16)
            pieces[pl.ds(pl.multiple_of(b * lev, 2 * lev), 2 * lev), :] = both

    pl.semaphore_wait(barrier, n_space - 1 + n_member - 1)

    def space_copy(src, dst, d, phase):
        return pltpu.make_async_remote_copy(
            src_ref=src,
            dst_ref=dst,
            send_sem=send_sem.at[phase],
            recv_sem=recv_sem.at[phase],
            device_id={"space": d},
            device_id_type=MESH,
        )

    def member_copy(src, dst, d, phase):
        return pltpu.make_async_remote_copy(
            src_ref=src,
            dst_ref=dst,
            send_sem=send_sem.at[phase],
            recv_sem=recv_sem.at[phase],
            device_id={"member": d},
            device_id_type=MESH,
        )

    def send_idx(k, carry):
        d = lax.rem(me + k, n_space)
        space_copy(idx_send.at[d], idx_recv.at[me], d, 0).start()
        return carry

    lax.fori_loop(1, n_space, send_idx, 0)

    per_step = 4
    step_rows = per_step * rows
    packed = pieces[...]

    def place(k, carry):
        first = lax.rem((me // per_step + k) * per_step, n_space)
        row = iota((step_rows, fine_rows), 0).astype(F32)
        wanted = place_row - (first * rows).astype(F32)
        values = dot(one_hot(row == wanted), packed).astype(BF16)
        for q in range(per_step):
            d = first + q
            send[d] = values[q * rows : (q + 1) * rows, :]

            @pl.when(d != me)
            def _():
                space_copy(send.at[d], recv.at[me], d, 1).start()

        return carry

    lax.fori_loop(1, n_space // per_step + 1, place, 0)
    recv[me] = send[me]
    idx_recv[me] = idx_send[me]

    widen_col = one_hot(iota((fine_rows, fine_count), 0) // lev == iota((fine_rows, fine_count), 1))
    slot_wide = jnp.broadcast_to(slot_col, (fine_count, 128)).astype(BF16)
    place_col = dot(widen_col, slot_wide) * lev + (iota((fine_rows, 128), 0) % lev).astype(F32)
    for t in range(slots // 128):
        unplace[:, t * 128 : (t + 1) * 128] = one_hot(
            place_col == (iota((fine_rows, 128), 1) + t * 128).astype(F32)
        )

    idx_all = space_copy(
        idx_send.at[pl.ds(0, n_space - 1)],
        idx_recv.at[pl.ds(0, n_space - 1)],
        lax.rem(me + 1, n_space),
        0,
    )
    idx_all.wait_recv()
    index = jnp.concatenate([idx_recv[s] for s in range(n_space)], axis=0).astype(BF16)
    lane_rank = one_hot((iota((128, slots), 1) % rows) // lev == iota((128, slots), 0))
    by_source = dot(index, lane_rank)
    mine = iota((n_space, slots), 1) // rows == iota((n_space, slots), 0)
    index_row = jnp.sum(jnp.where(mine, by_source, 0.0), axis=0, keepdims=True)
    index_row = (index_row - 1.0) * lev + (iota((1, slots), 1) % lev).astype(F32)
    collect[...] = one_hot(iota((coarse_rows, slots), 0).astype(F32) == index_row)
    source_of = one_hot(iota((slots, n_space), 0) // rows == iota((slots, n_space), 1))
    by_row = dot(source_of, index)
    rank_of = (iota((slots, 128), 0) % rows) // lev == iota((slots, 128), 1)
    index_col = jnp.sum(jnp.where(rank_of, by_row, 0.0), axis=1, keepdims=True)
    index_col = (index_col - 1.0) * lev + (iota((slots, 1), 0) % lev).astype(F32)
    spread[...] = one_hot(iota((slots, coarse_rows), 1).astype(F32) == index_col)

    mix = lax.dot_general(
        modes_ref[...],
        modes_ref[...],
        (((1,), (1,)), ((), ())),
        precision=lax.Precision.HIGHEST,
        preferred_element_type=F32,
    )
    mix_high = mix.astype(BF16)
    mix_low = (mix - mix_high.astype(F32)).astype(BF16)
    mix_both = jnp.concatenate([mix_high, mix_low], axis=1)

    space_copy(
        send.at[pl.ds(0, n_space - 1)],
        recv.at[pl.ds(0, n_space - 1)],
        lax.rem(me + 1, n_space),
        1,
    ).wait_recv()
    restricted = dot(collect[...], recv[...].reshape(slots, width)).astype(BF16)
    levels_buf[group] = restricted

    def send_levels(k, carry):
        d = lax.rem(group + k, n_member)
        member_copy(levels_buf.at[group], levels_buf.at[group], d, 2).start()
        return carry

    lax.fori_loop(1, n_member, send_levels, 0)
    ens_copy.wait()
    member_copy(
        levels_buf.at[pl.ds(0, n_member - 1)],
        levels_buf.at[pl.ds(0, n_member - 1)],
        lax.rem(group + 1, n_member),
        2,
    ).wait_recv()

    def coarse_pair(i, carry):
        at = pl.multiple_of(i * 2 * lev, 2 * lev)
        slabs = [levels_buf[g, pl.ds(at, 2 * lev), :].astype(F32) for g in range(n_member)]
        totals = []
        for half in range(2):
            c = i * 2 + half
            here = jnp.concatenate(
                [slab[half * lev : (half + 1) * lev] for slab in slabs], axis=0
            ).astype(BF16)
            schur = jnp.concatenate([ens[m, c] * here for m in range(members)], axis=1)
            rebuilt = dot(mix_both, jnp.concatenate([schur, schur], axis=0))
            total = jnp.zeros(here.shape, F32)
            for m in range(members):
                total += ens[m, c].astype(F32) * rebuilt[:, m * width : (m + 1) * width]
            totals.append(total)
        for g in range(n_member):
            contrib[g, pl.ds(at, 2 * lev), :] = jnp.concatenate(
                [total[g * lev : (g + 1) * lev] for total in totals], axis=0
            ).astype(BF16)
        return carry

    lax.fori_loop(0, coarse // 2, coarse_pair, 0)

    def send_contrib(k, carry):
        d = lax.rem(group + k, n_member)
        member_copy(contrib.at[d], arrived.at[group], d, 3).start()
        return carry

    lax.fori_loop(1, n_member, send_contrib, 0)
    arrived[group] = contrib[group]
    member_copy(
        contrib.at[pl.ds(0, n_member - 1)],
        arrived.at[pl.ds(0, n_member - 1)],
        lax.rem(group + 1, n_member),
        3,
    ).wait_recv()
    applied = arrived[0].astype(F32)
    for g in range(1, n_member):
        applied += arrived[g].astype(F32)
    applied = (applied / scale).astype(BF16)

    def answer(k, carry):
        first = lax.rem((me // per_step + k) * per_step, n_space)
        at = pl.multiple_of(first * rows, step_rows)
        values = dot(spread[pl.ds(at, step_rows), :], applied).astype(BF16)
        for q in range(per_step):
            d = first + q
            reply[d] = values[q * rows : (q + 1) * rows, :]

            @pl.when(d != me)
            def _():
                space_copy(reply.at[d], back.at[me], d, 4).start()

        return carry

    lax.fori_loop(1, n_space // per_step + 1, answer, 0)
    back[me] = reply[me]
    space_copy(
        reply.at[pl.ds(0, n_space - 1)],
        back.at[pl.ds(0, n_space - 1)],
        lax.rem(me + 1, n_space),
        4,
    ).wait_recv()
    fine[...] = dot(unplace[...], back[...].reshape(slots, width)).astype(BF16)

    @pl.loop(0, fine_count // 2, unroll=4)
    def _(i):
        b = i * 2
        both = fine[pl.ds(pl.multiple_of(b * lev, 2 * lev), 2 * lev), :]
        for half in range(2):
            out_ref[b + half] = lax.dot_general(
                both[half * lev : (half + 1) * lev],
                interp[b + half],
                (((1,), (1,)), ((), ())),
                preferred_element_type=F32,
            )

    def sent(src, d, make, phase):
        make(src, src, d, phase).wait_send()

    other = lax.rem(me + 1, n_space)
    sent(idx_send.at[pl.ds(0, n_space - 1)], other, space_copy, 0)
    sent(send.at[pl.ds(0, n_space - 1)], other, space_copy, 1)
    sent(levels_buf.at[pl.ds(0, n_member - 1)], lax.rem(group + 1, n_member), member_copy, 2)
    sent(contrib.at[pl.ds(0, n_member - 1)], lax.rem(group + 1, n_member), member_copy, 3)
    sent(reply.at[pl.ds(0, n_space - 1)], other, space_copy, 4)


def on_device(increment, interp, owner, local_block, ensemble, modes):
    fine_count, lev, width = increment.shape
    members, coarse, all_lev, _ = ensemble.shape
    n_space, n_member = lax.axis_size("space"), lax.axis_size("member")
    chunks = 6
    scale = float(members * n_member - 1)
    dims = (n_space, n_member, fine_count, lev, members, coarse, width, chunks, scale)
    rows = CAP * lev
    slots = n_space * rows
    anywhere = pl.BlockSpec(memory_space=pl.ANY)
    vmem = pl.BlockSpec(memory_space=pltpu.VMEM)
    exchange = pltpu.VMEM((n_space, rows, width), BF16)
    by_group = pltpu.VMEM((n_member, coarse * lev, width), BF16)
    return pl.pallas_call(
        functools.partial(kernel, dims),
        out_shape=jax.ShapeDtypeStruct((fine_count, lev, width), F32),
        in_specs=[anywhere, anywhere, anywhere, vmem, vmem, vmem],
        out_specs=vmem,
        scratch_shapes=[
            pltpu.VMEM(interp.shape, BF16),
            pltpu.VMEM(increment.shape, BF16),
            pltpu.VMEM(ensemble.shape, BF16),
            pltpu.VMEM((fine_count * lev, width), BF16),
            exchange,
            exchange,
            pltpu.VMEM((n_space, 1, 128), F32),
            pltpu.VMEM((n_space, 1, 128), F32),
            pltpu.VMEM((fine_count * lev, slots), BF16),
            pltpu.VMEM((coarse * lev, slots), BF16),
            pltpu.VMEM((slots, coarse * lev), BF16),
            by_group,
            by_group,
            by_group,
            exchange,
            exchange,
            pltpu.VMEM((fine_count * lev, width), BF16),
            pltpu.SemaphoreType.DMA((chunks + 2,)),
            pltpu.SemaphoreType.DMA((5,)),
            pltpu.SemaphoreType.DMA((5,)),
        ],
        compiler_params=pltpu.CompilerParams(
            collective_id=0, has_side_effects=True, vmem_limit_bytes=48 * 1024 * 1024
        ),
        name="covariance_apply",
    )(interp, increment, ensemble, owner, local_block.reshape(1, fine_count), modes)


def solution(mesh):
    in_specs = (
        P("space", "member", None),
        P("space", None, None),
        P("space", None),
        P("space"),
        P("member", "space", None, None),
        P(),
    )
    out_specs = P("space", "member", None)
    return jax.shard_map(
        on_device, mesh=mesh, in_specs=in_specs, out_specs=out_specs, check_vma=False
    )
```

time: 169 us -> 62 us (0.37); the launches traced: 166 us -> 61.8 us
  matrix products: 56.9 us -> 0 us
  Pallas kernels: 0 us -> 56.1 us
  blocking collectives: 36.9 us -> 0 us
  waiting for transfers between devices: 36.7 us -> 0 us
  starting transfers between devices: 19.6 us -> 0 us
  other arithmetic: 6.58 us -> 0 us
  local copies, waits for them, and re-layouts: 9.32 us -> 5.74 us
    dot_general x27 -> x0, matrix products: 56.9 us -> none  [the longest x10 30.2 us: member_step(): rebuilt = jnp.einsum('ckj,lk->clj', coefficients, modes, precision=highest)]
    pallas_call x0 -> x1, Pallas kernels: none -> 56.1 us  [on_device(): pl.pallas_call(functools.partial(kernel, dims), out_shape=jax.ShapeDtypeS...]
    all_to_all x2 -> x0, blocking collectives: 36.9 us -> none  [the longest x1 20.8 us: on_device(): lax.all_to_all(reply, 'space', split_axis=0, concat_axis=0, tiled=True)]
    all_to_all x2 -> x0, waiting for transfers between devices: 36.7 us -> none  [the longest x1 28.6 us: sent_together(): lax.all_to_all(both, axis, split_axis=split_dim, concat_axis=concat_dim,...]
    all_to_all x2 -> x0, starting transfers between devices: 19.6 us -> none  [the longest x1 12.1 us: sent_together(): lax.all_to_all(both, axis, split_axis=split_dim, concat_axis=concat_dim,...]
    unnamed x8 -> x9, local copies, waits for them, and re-layouts: 0.05 us -> 5.74 us
    all_to_all x3 -> x0, local copies, waits for them, and re-layouts: 4.47 us -> none  [the longest x1 2.37 us: sent_together(): lax.all_to_all(both, axis, split_axis=split_dim, concat_axis=concat_dim,...]
    reduce_sum x2 -> x0, other arithmetic: 2.64 us -> none  [the longest x1 1.81 us: summed_on_arrival(): return jnp.sum(parts, axis=0)]
  transfers between devices with their start and end apart: 2 -> 0, of which waited for: 2 -> 0; matrix products, arithmetic and copies ran while one was open for 0% -> 0% of each run, Pallas kernels for 0% -> 0%
where the time goes in v1:
time: 62 us; the launch traced here: 61.8 us
  Pallas kernels  56.1 us (90%)
  local copies, waits for them, and re-layouts  5.74 us (9%)
    pallas_call x1, Pallas kernels, on_device(): pl.pallas_call(functools.partial(kernel, dims), out_shape=jax.ShapeDtypeS...  56.1 us
    unnamed x9, local copies, waits for them, and re-layouts  5.74 us

profile of v1, /device:TPU:1, one launch (start us, length us, event | category | flops | bytes accessed | tf_op | source)
XLA Modules:
  0.0 61.8 jit_solution(13886750096836271730)
XLA Ops:
  0.0 0.8 %copy.8.modes_ref = f32[64,4]{1,0:T(8,128)S(1)} copy(f32[64,4]{0,1:T(4,128)} %param.11) | data formatting | bytes 2048 | tf_op args[5]
  0.8 0.8 %copy.7.owner_ref = s32[96,1]{1,0:T(8,128)S(1)} copy(s32[96,1]{0,1:T(1,128)} %param.8) | data formatting | bytes 768 | tf_op args[2]
  1.5 0.0 copy-start
  1.5 1.9 %copy-done = bf16[96,128,128]{2,1,0:T(8,128)(2,1)S(1)} copy-done((bf16[96,128,128]{2,1,0:T(8,128)(2,1)S(1)}, bf16[96,128,128]{2,1,0:T(8,128)(2,1)}, u32[]{:S(2)}) %copy-start) | copy-done | bytes 3145752
  3.4 0.0 copy-start.1
  3.4 0.9 %copy-done.1 = bf16[96,8,128]{2,1,0:T(8,128)(2,1)S(1)} copy-done((bf16[96,8,128]{2,1,0:T(8,128)(2,1)S(1)}, bf16[96,8,128]{2,1,0:T(8,128)(2,1)}, u32[]{:S(2)}) %copy-start.1) | copy-done | bytes 196632
  4.3 0.0 copy-start.2
  4.3 0.7 %copy-done.2 = s32[96]{0:T(128)S(1)} copy-done((s32[96]{0:T(128)S(1)}, s32[96]{0:T(128)}, u32[]{:S(2)}) %copy-start.2) | copy-done | bytes 408
  5.0 56.1 %covariance_apply.1 = f32[96,8,128]{2,1,0:T(8,128)S(1)} custom-call(bf16[96,128,128]{2,1,0:T(8,128)(2,1)S(1)} %copy-done, bf16[96,8,128]{2,1,0:T(8,128)(2,1)S(1)} %copy-done.1, bf16[10,24,64,128]{3,2,1,0:T(8,128)(2,1)} %ens_hbm.1, s32[96,1]{1,0:T(8,128)S(1)} %copy.7.owner_ref, s32[1,96]{1,0:T(1,128)S(1)} %bitcast.1, f32[64,4]{1,0:T(8,128)S(1)} %copy.8.modes_ref), custom_call_target="tpu_custom_call" | custom-call | tf_op jit(solution)/shard_map/covariance_apply/pallas_call | solution.py:343
  61.1 0.7 %copy.10 = f32[96,8,128]{2,1,0:T(8,128)} copy(f32[96,8,128]{2,1,0:T(8,128)S(1)} %covariance_apply.1) | data formatting | bytes 786432
Async XLA Ops:
  1.5 1.9 %copy-start = (bf16[96,128,128]{2,1,0:T(8,128)(2,1)S(1)}, bf16[96,128,128]{2,1,0:T(8,128)(2,1)}, u32[]{:S(2)}) copy-start(bf16[96,128,128]{2,1,0:T(8,128)(2,1)} %interp_hbm.1) | copy-start | bytes 9437188
  3.4 0.9 %copy-start.1 = (bf16[96,8,128]{2,1,0:T(8,128)(2,1)S(1)}, bf16[96,8,128]{2,1,0:T(8,128)(2,1)}, u32[]{:S(2)}) copy-start(bf16[96,8,128]{2,1,0:T(8,128)(2,1)} %inc_hbm.1) | copy-start | bytes 589828
  4.3 0.7 %copy-start.2 = (s32[96]{0:T(128)S(1)}, s32[96]{0:T(128)}, u32[]{:S(2)}) copy-start(s32[96]{0:T(128)} %param.9) | copy-start | bytes 1156

commit v2 on v1

--- a/solution.py
+++ b/solution.py
@@ -29,10 +29,13 @@
     interp_hbm,
     inc_hbm,
     ens_hbm,
+    owner_hbm,
+    local_hbm,
+    modes_hbm,
+    out_ref,
     owner_ref,
     local_ref,
     modes_ref,
-    out_ref,
     interp,
     inc,
     ens,
@@ -54,7 +57,7 @@
     send_sem,
     recv_sem,
 ):
-    n_space, n_member, fine_count, lev, members, coarse, width, chunks, scale = dims
+    n_space, n_member, fine_count, lev, members, coarse, width, chunks, parts, n_y, scale = dims
     rows = CAP * lev
     slots = n_space * rows
     fine_rows = fine_count * lev
@@ -63,16 +66,42 @@
     group = lax.axis_index("member")
     per = fine_count // chunks
 
-    inc_copy = pltpu.make_async_copy(inc_hbm, inc, load_sem.at[chunks])
-    inc_copy.start()
+    def load(src, dst, i):
+        copy = pltpu.make_async_copy(src, dst, load_sem.at[i])
+        copy.start()
+        return copy
+
+    owner_copy = load(owner_hbm, owner_ref, chunks + 2)
+    local_copy = load(local_hbm, local_ref, chunks + 3)
+    inc_copy = load(inc_hbm, inc, chunks)
     loads = []
     for t in range(chunks):
         part = pl.ds(t * per, per)
-        copy = pltpu.make_async_copy(interp_hbm.at[part], interp.at[part], load_sem.at[t])
-        copy.start()
-        loads.append(copy)
-    ens_copy = pltpu.make_async_copy(ens_hbm, ens, load_sem.at[chunks + 1])
-    ens_copy.start()
+        loads.append(load(interp_hbm.at[part], interp.at[part], t))
+    modes_copy = load(modes_hbm, modes_ref, chunks + 4)
+
+    last = n_space - 1
+    n_z = n_space // n_y
+    my_z, my_y = me // n_y, lax.rem(me, n_y)
+
+    def peer_at(p):
+        k = last - p
+        k_y, k_z = k // n_z, lax.rem(k, n_z)
+        half = (k_z + 1) // 2
+        up = lax.rem(k_z, 2) == 1
+        step_z = jnp.where(up, half, n_z - half)
+        device = lax.rem(my_z + step_z, n_z) * n_y + lax.rem(my_y + k_y, n_y)
+        paired = (k_z == 0) | (k_z == n_z - 1)
+        back_z = jnp.where(paired, k_z, jnp.where(up, k_z + 1, k_z - 1))
+        return device, last - (lax.rem(n_y - k_y, n_y) * n_z + back_z)
+
+    def position_of(device):
+        step_z = (device // n_y - my_z + n_z) % n_z
+        step_y = (device % n_y - my_y + n_y) % n_y
+        k_z = jnp.where(
+            step_z <= n_z // 2, jnp.maximum(2 * step_z - 1, 0), 2 * (n_z - step_z)
+        )
+        return last - (step_y * n_z + k_z)
 
     barrier = pltpu.get_barrier_semaphore()
 
@@ -89,11 +118,12 @@
     lax.fori_loop(1, n_space, greet_space, 0)
     lax.fori_loop(1, n_member, greet_member, 0)
 
-    owner_col = owner_ref[...].astype(F32)
-    own_b = jnp.broadcast_to(owner_col, (fine_count, fine_count))
+    owner_copy.wait()
+    local_copy.wait()
+    owner_row = position_of(owner_ref[...]).astype(F32)
     down, across = iota((fine_count, fine_count), 0), iota((fine_count, fine_count), 1)
-    owner_row = jnp.sum(jnp.where(down == across, own_b, 0.0), axis=0, keepdims=True)
-    same = own_b == owner_row
+    owner_col = jnp.sum(jnp.where(down == across, owner_row, 0.0), axis=1, keepdims=True)
+    same = owner_col == owner_row
     rank_row = jnp.sum(jnp.where(same & (down < across), 1.0, 0.0), axis=0, keepdims=True)
     rank_col = jnp.sum(jnp.where(same & (across < down), 1.0, 0.0), axis=1, keepdims=True)
     slot_row = owner_row * CAP + rank_row
@@ -124,6 +154,7 @@
             both = jnp.concatenate([first, second], axis=0).astype(BF16)
             pieces[pl.ds(pl.multiple_of(b * lev, 2 * lev), 2 * lev), :] = both
 
+    ens_copy = load(ens_hbm, ens, chunks + 1)
     pl.semaphore_wait(barrier, n_space - 1 + n_member - 1)
 
     def space_copy(src, dst, d, phase):
@@ -147,34 +178,34 @@
         )
 
     def send_idx(k, carry):
-        d = lax.rem(me + k, n_space)
-        space_copy(idx_send.at[d], idx_recv.at[me], d, 0).start()
+        d, there = peer_at(k)
+        space_copy(idx_send.at[k], idx_recv.at[there], d, 0).start()
         return carry
 
-    lax.fori_loop(1, n_space, send_idx, 0)
+    lax.fori_loop(0, last, send_idx, 0)
 
     per_step = 4
     step_rows = per_step * rows
     packed = pieces[...]
 
     def place(k, carry):
-        first = lax.rem((me // per_step + k) * per_step, n_space)
         row = iota((step_rows, fine_rows), 0).astype(F32)
-        wanted = place_row - (first * rows).astype(F32)
+        wanted = place_row - (k * step_rows).astype(F32)
         values = dot(one_hot(row == wanted), packed).astype(BF16)
         for q in range(per_step):
-            d = first + q
-            send[d] = values[q * rows : (q + 1) * rows, :]
-
-            @pl.when(d != me)
+            p = k * per_step + q
+            send[p] = values[q * rows : (q + 1) * rows, :]
+
+            @pl.when(p != last)
             def _():
-                space_copy(send.at[d], recv.at[me], d, 1).start()
+                d, there = peer_at(p)
+                space_copy(send.at[p], recv.at[there], d, 1).start()
 
         return carry
 
-    lax.fori_loop(1, n_space // per_step + 1, place, 0)
-    recv[me] = send[me]
-    idx_recv[me] = idx_send[me]
+    lax.fori_loop(0, n_space // per_step, place, 0)
+    recv[last] = send[last]
+    idx_recv[last] = idx_send[last]
 
     widen_col = one_hot(iota((fine_rows, fine_count), 0) // lev == iota((fine_rows, fine_count), 1))
     slot_wide = jnp.broadcast_to(slot_col, (fine_count, 128)).astype(BF16)
@@ -205,10 +236,11 @@
     index_col = (index_col - 1.0) * lev + (iota((slots, 1), 0) % lev).astype(F32)
     spread[...] = one_hot(iota((slots, coarse_rows), 1).astype(F32) == index_col)
 
+    modes_copy.wait()
     mix = lax.dot_general(
         modes_ref[...],
         modes_ref[...],
-        (((1,), (1,)), ((), ())),
+        (((0,), (0,)), ((), ())),
         precision=lax.Precision.HIGHEST,
         preferred_element_type=F32,
     )
@@ -223,84 +255,92 @@
         1,
     ).wait_recv()
     restricted = dot(collect[...], recv[...].reshape(slots, width)).astype(BF16)
-    levels_buf[group] = restricted
-
-    def send_levels(k, carry):
-        d = lax.rem(group + k, n_member)
-        member_copy(levels_buf.at[group], levels_buf.at[group], d, 2).start()
-        return carry
-
-    lax.fori_loop(1, n_member, send_levels, 0)
+    part_rows = coarse_rows // parts
+    for q in range(parts):
+        levels_buf[q, group] = restricted[q * part_rows : (q + 1) * part_rows]
+
+        def send_levels(k, carry):
+            d = lax.rem(group + k, n_member)
+            member_copy(levels_buf.at[q, group], levels_buf.at[q, group], d, 2 + q).start()
+            return carry
+
+        lax.fori_loop(1, n_member, send_levels, 0)
     ens_copy.wait()
-    member_copy(
-        levels_buf.at[pl.ds(0, n_member - 1)],
-        levels_buf.at[pl.ds(0, n_member - 1)],
-        lax.rem(group + 1, n_member),
-        2,
-    ).wait_recv()
-
-    def coarse_pair(i, carry):
-        at = pl.multiple_of(i * 2 * lev, 2 * lev)
-        slabs = [levels_buf[g, pl.ds(at, 2 * lev), :].astype(F32) for g in range(n_member)]
-        totals = []
-        for half in range(2):
-            c = i * 2 + half
-            here = jnp.concatenate(
-                [slab[half * lev : (half + 1) * lev] for slab in slabs], axis=0
-            ).astype(BF16)
-            schur = jnp.concatenate([ens[m, c] * here for m in range(members)], axis=1)
-            rebuilt = dot(mix_both, jnp.concatenate([schur, schur], axis=0))
-            total = jnp.zeros(here.shape, F32)
-            for m in range(members):
-                total += ens[m, c].astype(F32) * rebuilt[:, m * width : (m + 1) * width]
-            totals.append(total)
-        for g in range(n_member):
-            contrib[g, pl.ds(at, 2 * lev), :] = jnp.concatenate(
-                [total[g * lev : (g + 1) * lev] for total in totals], axis=0
-            ).astype(BF16)
-        return carry
-
-    lax.fori_loop(0, coarse // 2, coarse_pair, 0)
-
-    def send_contrib(k, carry):
-        d = lax.rem(group + k, n_member)
-        member_copy(contrib.at[d], arrived.at[group], d, 3).start()
-        return carry
-
-    lax.fori_loop(1, n_member, send_contrib, 0)
-    arrived[group] = contrib[group]
-    member_copy(
-        contrib.at[pl.ds(0, n_member - 1)],
-        arrived.at[pl.ds(0, n_member - 1)],
-        lax.rem(group + 1, n_member),
-        3,
-    ).wait_recv()
-    applied = arrived[0].astype(F32)
-    for g in range(1, n_member):
-        applied += arrived[g].astype(F32)
-    applied = (applied / scale).astype(BF16)
+
+    others = pl.ds(0, n_member - 1)
+    next_member = lax.rem(group + 1, n_member)
+    for q in range(parts):
+        member_copy(
+            levels_buf.at[q, others], levels_buf.at[q, others], next_member, 2 + q
+        ).wait_recv()
+
+        def coarse_pair(i, carry):
+            at = pl.multiple_of(i * 2 * lev, 2 * lev)
+            slabs = [
+                levels_buf[q, g, pl.ds(at, 2 * lev), :].astype(F32) for g in range(n_member)
+            ]
+            totals = []
+            for half in range(2):
+                c = q * (coarse // parts) + i * 2 + half
+                here = jnp.concatenate(
+                    [slab[half * lev : (half + 1) * lev] for slab in slabs], axis=0
+                ).astype(BF16)
+                schur = jnp.concatenate([ens[m, c] * here for m in range(members)], axis=1)
+                rebuilt = dot(mix_both, jnp.concatenate([schur, schur], axis=0))
+                total = jnp.zeros(here.shape, F32)
+                for m in range(members):
+                    total += ens[m, c].astype(F32) * rebuilt[:, m * width : (m + 1) * width]
+                totals.append(total)
+            for g in range(n_member):
+                contrib[q, g, pl.ds(at, 2 * lev), :] = jnp.concatenate(
+                    [total[g * lev : (g + 1) * lev] for total in totals], axis=0
+                ).astype(BF16)
+            return carry
+
+        lax.fori_loop(0, coarse // parts // 2, coarse_pair, 0)
+
+        def send_contrib(k, carry):
+            d = lax.rem(group + k, n_member)
+            member_copy(
+                contrib.at[q, d], arrived.at[q, group], d, 2 + parts + q
+            ).start()
+            return carry
+
+        lax.fori_loop(1, n_member, send_contrib, 0)
+        arrived[q, group] = contrib[q, group]
+
+    summed = []
+    for q in range(parts):
+        member_copy(
+            contrib.at[q, others], arrived.at[q, others], next_member, 2 + parts + q
+        ).wait_recv()
+        total = arrived[q, 0].astype(F32)
+        for g in range(1, n_member):
+            total += arrived[q, g].astype(F32)
+        summed.append((total / scale).astype(BF16))
+    applied = jnp.concatenate(summed, axis=0)
 
     def answer(k, carry):
-        first = lax.rem((me // per_step + k) * per_step, n_space)
-        at = pl.multiple_of(first * rows, step_rows)
+        at = pl.multiple_of(k * step_rows, step_rows)
         values = dot(spread[pl.ds(at, step_rows), :], applied).astype(BF16)
         for q in range(per_step):
-            d = first + q
-            reply[d] = values[q * rows : (q + 1) * rows, :]
-
-            @pl.when(d != me)
+            p = k * per_step + q
+            reply[p] = values[q * rows : (q + 1) * rows, :]
+
+            @pl.when(p != last)
             def _():
-                space_copy(reply.at[d], back.at[me], d, 4).start()
+                d, there = peer_at(p)
+                space_copy(reply.at[p], back.at[there], d, 2 + 2 * parts).start()
 
         return carry
 
-    lax.fori_loop(1, n_space // per_step + 1, answer, 0)
-    back[me] = reply[me]
+    lax.fori_loop(0, n_space // per_step, answer, 0)
+    back[last] = reply[last]
     space_copy(
         reply.at[pl.ds(0, n_space - 1)],
         back.at[pl.ds(0, n_space - 1)],
         lax.rem(me + 1, n_space),
-        4,
+        2 + 2 * parts,
     ).wait_recv()
     fine[...] = dot(unplace[...], back[...].reshape(slots, width)).astype(BF16)
 
@@ -322,9 +362,10 @@
     other = lax.rem(me + 1, n_space)
     sent(idx_send.at[pl.ds(0, n_space - 1)], other, space_copy, 0)
     sent(send.at[pl.ds(0, n_space - 1)], other, space_copy, 1)
-    sent(levels_buf.at[pl.ds(0, n_member - 1)], lax.rem(group + 1, n_member), member_copy, 2)
-    sent(contrib.at[pl.ds(0, n_member - 1)], lax.rem(group + 1, n_member), member_copy, 3)
-    sent(reply.at[pl.ds(0, n_space - 1)], other, space_copy, 4)
+    for q in range(parts):
+        sent(levels_buf.at[q, others], next_member, member_copy, 2 + q)
+        sent(contrib.at[q, others], next_member, member_copy, 2 + parts + q)
+    sent(reply.at[pl.ds(0, n_space - 1)], other, space_copy, 2 + 2 * parts)
 
 
 def on_device(increment, interp, owner, local_block, ensemble, modes):
@@ -333,19 +374,33 @@
     n_space, n_member = lax.axis_size("space"), lax.axis_size("member")
     chunks = 6
     scale = float(members * n_member - 1)
-    dims = (n_space, n_member, fine_count, lev, members, coarse, width, chunks, scale)
+    parts, n_y = 4, 4
+    dims = (
+        n_space, n_member, fine_count, lev, members, coarse, width, chunks, parts, n_y, scale
+    )
     rows = CAP * lev
     slots = n_space * rows
-    anywhere = pl.BlockSpec(memory_space=pl.ANY)
+    arguments = (
+        interp,
+        increment,
+        ensemble,
+        owner.reshape(1, fine_count),
+        local_block.reshape(1, fine_count),
+        modes.T,
+    )
+    hbm = pl.BlockSpec(memory_space=pltpu.HBM)
     vmem = pl.BlockSpec(memory_space=pltpu.VMEM)
     exchange = pltpu.VMEM((n_space, rows, width), BF16)
-    by_group = pltpu.VMEM((n_member, coarse * lev, width), BF16)
+    by_group = pltpu.VMEM((parts, n_member, coarse // parts * lev, width), BF16)
     return pl.pallas_call(
         functools.partial(kernel, dims),
         out_shape=jax.ShapeDtypeStruct((fine_count, lev, width), F32),
-        in_specs=[anywhere, anywhere, anywhere, vmem, vmem, vmem],
+        in_specs=[hbm] * 6,
         out_specs=vmem,
         scratch_shapes=[
+            pltpu.VMEM((1, fine_count), jnp.int32),
+            pltpu.VMEM((1, fine_count), jnp.int32),
+            pltpu.VMEM(modes.shape[::-1], F32),
             pltpu.VMEM(interp.shape, BF16),
             pltpu.VMEM(increment.shape, BF16),
             pltpu.VMEM(ensemble.shape, BF16),
@@ -363,15 +418,15 @@
             exchange,
             exchange,
             pltpu.VMEM((fine_count * lev, width), BF16),
-            pltpu.SemaphoreType.DMA((chunks + 2,)),
-            pltpu.SemaphoreType.DMA((5,)),
-            pltpu.SemaphoreType.DMA((5,)),
+            pltpu.SemaphoreType.DMA((chunks + 5,)),
+            pltpu.SemaphoreType.DMA((3 + 2 * parts,)),
+            pltpu.SemaphoreType.DMA((3 + 2 * parts,)),
         ],
         compiler_params=pltpu.CompilerParams(
             collective_id=0, has_side_effects=True, vmem_limit_bytes=48 * 1024 * 1024
         ),
         name="covariance_apply",
-    )(interp, increment, ensemble, owner, local_block.reshape(1, fine_count), modes)
+    )(*[pltpu.with_memory_space_constraint(a, pltpu.HBM) for a in arguments])
 
 
 def solution(mesh):

time: 62 us -> 50.2 us (0.81)
  Pallas kernels: 56.1 us -> 49.4 us
  local copies, waits for them, and re-layouts: 5.74 us -> 0.75 us
    pallas_call x1, Pallas kernels: 56.1 us -> 49.4 us  [on_device(): pl.pallas_call(functools.partial(kernel, dims), out_shape=jax.ShapeDtypeS...]
    unnamed x9 -> x1, local copies, waits for them, and re-layouts: 5.74 us -> 0.75 us
where the time goes in v2:
time: 50.2 us
  Pallas kernels  49.4 us (98%)
  local copies, waits for them, and re-layouts  0.75 us (1%)
    pallas_call x1, Pallas kernels, on_device(): pl.pallas_call(functools.partial(kernel, dims), out_shape=jax.ShapeDtypeS...  49.4 us

profile of v2, /device:TPU:1, one launch (start us, length us, event | category | flops | bytes accessed | tf_op | source)
XLA Modules:
  0.0 50.2 jit_solution(11515686249410307639)
XLA Ops:
  0.0 49.4 %covariance_apply.1 = f32[96,8,128]{2,1,0:T(8,128)S(1)} custom-call(bf16[96,128,128]{2,1,0:T(8,128)(2,1)} %interp_hbm.1, bf16[96,8,128]{2,1,0:T(8,128)(2,1)} %inc_hbm.1, bf16[10,24,64,128]{3,2,1,0:T(8,128)(2,1)} %ens_hbm.1, s32[1,96]{1,0:T(1,128)} %bitcast.4, s32[1,96]{1,0:T(1,128)} %bitcast.5, f32[4,64]{1,0:T(4,128)} %bitcast.3), custom_call_target="tpu_custom_call" | custom-call | tf_op jit(solution)/shard_map/covariance_apply/pallas_call | solution.py:395
  49.4 0.7 %copy.8 = f32[96,8,128]{2,1,0:T(8,128)} copy(f32[96,8,128]{2,1,0:T(8,128)S(1)} %covariance_apply.1) | data formatting | bytes 786432

commit v3 on v2

--- a/solution.py
+++ b/solution.py
@@ -44,6 +44,7 @@
     recv,
     idx_send,
     idx_recv,
+    placing,
     unplace,
     collect,
     spread,
@@ -66,6 +67,21 @@
     group = lax.axis_index("member")
     per = fine_count // chunks
 
+    barrier = pltpu.get_barrier_semaphore()
+
+    def greet_space(k, carry):
+        peer = {"space": lax.rem(me + k, n_space)}
+        pl.semaphore_signal(barrier, inc=1, device_id=peer, device_id_type=MESH)
+        return carry
+
+    def greet_member(k, carry):
+        peer = {"member": lax.rem(group + k, n_member)}
+        pl.semaphore_signal(barrier, inc=1, device_id=peer, device_id_type=MESH)
+        return carry
+
+    lax.fori_loop(1, n_space, greet_space, 0)
+    lax.fori_loop(1, n_member, greet_member, 0)
+
     def load(src, dst, i):
         copy = pltpu.make_async_copy(src, dst, load_sem.at[i])
         copy.start()
@@ -79,6 +95,14 @@
         part = pl.ds(t * per, per)
         loads.append(load(interp_hbm.at[part], interp.at[part], t))
     modes_copy = load(modes_hbm, modes_ref, chunks + 4)
+
+    def member_at(k):
+        third = lax.rem(k, 3)
+        step = jnp.where(third == 0, 2, jnp.where(third == 1, 1, 3))
+        step = jnp.where(k == n_member - 2, 0, step)
+        core = lax.rem(group, 2)
+        flip = (k < 3) | (k == n_member - 2)
+        return lax.rem(group // 2 + step, n_member // 2) * 2 + jnp.where(flip, 1 - core, core)
 
     last = n_space - 1
     n_z = n_space // n_y
@@ -103,21 +127,6 @@
         )
         return last - (step_y * n_z + k_z)
 
-    barrier = pltpu.get_barrier_semaphore()
-
-    def greet_space(k, carry):
-        peer = {"space": lax.rem(me + k, n_space)}
-        pl.semaphore_signal(barrier, inc=1, device_id=peer, device_id_type=MESH)
-        return carry
-
-    def greet_member(k, carry):
-        peer = {"member": lax.rem(group + k, n_member)}
-        pl.semaphore_signal(barrier, inc=1, device_id=peer, device_id_type=MESH)
-        return carry
-
-    lax.fori_loop(1, n_space, greet_space, 0)
-    lax.fori_loop(1, n_member, greet_member, 0)
-
     owner_copy.wait()
     local_copy.wait()
     owner_row = position_of(owner_ref[...]).astype(F32)
@@ -142,6 +151,12 @@
     place_row = dot(jnp.broadcast_to(slot_row, (8, fine_count)).astype(BF16), widen)[0:1]
     place_row = place_row * lev + (iota((1, fine_rows), 1) % lev).astype(F32)
 
+    per_step = 4
+    step_rows = per_step * rows
+    for k in range(n_space // per_step):
+        row = (iota((step_rows, fine_rows), 0) + k * step_rows).astype(F32)
+        placing[k * step_rows : (k + 1) * step_rows, :] = one_hot(row == place_row)
+
     inc_copy.wait()
     for t in range(chunks):
         loads[t].wait()
@@ -184,14 +199,11 @@
 
     lax.fori_loop(0, last, send_idx, 0)
 
-    per_step = 4
-    step_rows = per_step * rows
     packed = pieces[...]
 
     def place(k, carry):
-        row = iota((step_rows, fine_rows), 0).astype(F32)
-        wanted = place_row - (k * step_rows).astype(F32)
-        values = dot(one_hot(row == wanted), packed).astype(BF16)
+        at = pl.multiple_of(k * step_rows, step_rows)
+        values = dot(placing[pl.ds(at, step_rows), :], packed).astype(BF16)
         for q in range(per_step):
             p = k * per_step + q
             send[p] = values[q * rows : (q + 1) * rows, :]
@@ -206,14 +218,6 @@
     lax.fori_loop(0, n_space // per_step, place, 0)
     recv[last] = send[last]
     idx_recv[last] = idx_send[last]
-
-    widen_col = one_hot(iota((fine_rows, fine_count), 0) // lev == iota((fine_rows, fine_count), 1))
-    slot_wide = jnp.broadcast_to(slot_col, (fine_count, 128)).astype(BF16)
-    place_col = dot(widen_col, slot_wide) * lev + (iota((fine_rows, 128), 0) % lev).astype(F32)
-    for t in range(slots // 128):
-        unplace[:, t * 128 : (t + 1) * 128] = one_hot(
-            place_col == (iota((fine_rows, 128), 1) + t * 128).astype(F32)
-        )
 
     idx_all = space_copy(
         idx_send.at[pl.ds(0, n_space - 1)],
@@ -260,11 +264,23 @@
         levels_buf[q, group] = restricted[q * part_rows : (q + 1) * part_rows]
 
         def send_levels(k, carry):
-            d = lax.rem(group + k, n_member)
+            d = member_at(k)
             member_copy(levels_buf.at[q, group], levels_buf.at[q, group], d, 2 + q).start()
             return carry
 
-        lax.fori_loop(1, n_member, send_levels, 0)
+        lax.fori_loop(0, n_member - 1, send_levels, 0)
+    @pl.loop(0, fine_count, unroll=4)
+    def _(b):
+        interp[b] = interp[b].T
+
+    widen_col = one_hot(iota((fine_rows, fine_count), 0) // lev == iota((fine_rows, fine_count), 1))
+    slot_wide = jnp.broadcast_to(slot_col, (fine_count, 128)).astype(BF16)
+    place_col = dot(widen_col, slot_wide) * lev + (iota((fine_rows, 128), 0) % lev).astype(F32)
+    for t in range(slots // 128):
+        unplace[:, t * 128 : (t + 1) * 128] = one_hot(
+            place_col == (iota((fine_rows, 128), 1) + t * 128).astype(F32)
+        )
+
     ens_copy.wait()
 
     others = pl.ds(0, n_member - 1)
@@ -300,13 +316,13 @@
         lax.fori_loop(0, coarse // parts // 2, coarse_pair, 0)
 
         def send_contrib(k, carry):
-            d = lax.rem(group + k, n_member)
+            d = member_at(k)
             member_copy(
                 contrib.at[q, d], arrived.at[q, group], d, 2 + parts + q
             ).start()
             return carry
 
-        lax.fori_loop(1, n_member, send_contrib, 0)
+        lax.fori_loop(0, n_member - 1, send_contrib, 0)
         arrived[q, group] = contrib[q, group]
 
     summed = []
@@ -352,7 +368,7 @@
             out_ref[b + half] = lax.dot_general(
                 both[half * lev : (half + 1) * lev],
                 interp[b + half],
-                (((1,), (1,)), ((), ())),
+                (((1,), (0,)), ((), ())),
                 preferred_element_type=F32,
             )
 
@@ -409,6 +425,7 @@
             exchange,
             pltpu.VMEM((n_space, 1, 128), F32),
             pltpu.VMEM((n_space, 1, 128), F32),
+            pltpu.VMEM((slots, fine_count * lev), BF16),
             pltpu.VMEM((fine_count * lev, slots), BF16),
             pltpu.VMEM((coarse * lev, slots), BF16),
             pltpu.VMEM((slots, coarse * lev), BF16),

time: 50.2 us -> 48.9 us (0.974)
  Pallas kernels: 49.4 us -> 48 us
    pallas_call x1, Pallas kernels: 49.4 us -> 48 us  [on_device(): pl.pallas_call(functools.partial(kernel, dims), out_shape=jax.ShapeDtypeS...]
where the time goes in v3:
time: 48.9 us; the launch traced here: 48.8 us
  Pallas kernels  48 us (98%)
  local copies, waits for them, and re-layouts  0.75 us (2%)
    pallas_call x1, Pallas kernels, on_device(): pl.pallas_call(functools.partial(kernel, dims), out_shape=jax.ShapeDtypeS...  48 us

profile of v3, /device:TPU:1, one launch (start us, length us, event | category | flops | bytes accessed | tf_op | source)
XLA Modules:
  0.0 48.8 jit_solution(18212513782421225452)
XLA Ops:
  0.0 48.0 %covariance_apply.1 = f32[96,8,128]{2,1,0:T(8,128)S(1)} custom-call(bf16[96,128,128]{2,1,0:T(8,128)(2,1)} %interp_hbm.1, bf16[96,8,128]{2,1,0:T(8,128)(2,1)} %inc_hbm.1, bf16[10,24,64,128]{3,2,1,0:T(8,128)(2,1)} %ens_hbm.1, s32[1,96]{1,0:T(1,128)} %bitcast.4, s32[1,96]{1,0:T(1,128)} %bitcast.5, f32[4,64]{1,0:T(4,128)} %bitcast.3), custom_call_target="tpu_custom_call" | custom-call | tf_op jit(solution)/shard_map/covariance_apply/pallas_call | solution.py:411
  48.0 0.7 %copy.8 = f32[96,8,128]{2,1,0:T(8,128)} copy(f32[96,8,128]{2,1,0:T(8,128)S(1)} %covariance_apply.1) | data formatting | bytes 786432

commit v4 on v3

v4 whole, which is shorter than its diff:
```python
import functools
import jax
import jax.numpy as jnp
from jax import lax
from jax.experimental import pallas as pl
from jax.experimental.pallas import tpu as pltpu
from jax.sharding import PartitionSpec as P

MESH = pl.DeviceIdType.MESH
CAP = 6
F32 = jnp.float32
BF16 = jnp.bfloat16


def iota(shape, dim):
    return lax.broadcasted_iota(jnp.int32, shape, dim)


def dot(a, b):
    return jnp.dot(a, b, preferred_element_type=F32)


def one_hot(condition):
    return jnp.where(condition, 1.0, 0.0).astype(BF16)


def kernel(
    dims,
    interp_hbm,
    inc_hbm,
    ens_hbm,
    owner_hbm,
    local_hbm,
    modes_hbm,
    out_ref,
    owner_ref,
    local_ref,
    modes_ref,
    interp,
    inc,
    ens,
    pairs,
    pieces,
    send,
    recv,
    idx_send,
    idx_recv,
    placing,
    unplace,
    collect,
    spread,
    levels_buf,
    contrib,
    arrived,
    reply,
    back,
    fine,
    load_sem,
    send_sem,
    recv_sem,
):
    n_space, n_member, fine_count, lev, members, coarse, width, chunks, parts, n_y, scale = dims
    near = lev // 2
    wide = width // 2
    rows = CAP * near
    slots = n_space * rows
    fine_rows = fine_count * near
    coarse_rows = coarse * near
    me = lax.axis_index("space")
    group = lax.axis_index("member")
    per = fine_count // chunks

    barrier = pltpu.get_barrier_semaphore()

    def greet_space(k, carry):
        peer = {"space": lax.rem(me + k, n_space)}
        pl.semaphore_signal(barrier, inc=1, device_id=peer, device_id_type=MESH)
        return carry

    def greet_member(k, carry):
        peer = {"member": lax.rem(group + k, n_member)}
        pl.semaphore_signal(barrier, inc=1, device_id=peer, device_id_type=MESH)
        return carry

    lax.fori_loop(1, n_space, greet_space, 0)
    lax.fori_loop(1, n_member, greet_member, 0)

    def load(src, dst, i):
        copy = pltpu.make_async_copy(src, dst, load_sem.at[i])
        copy.start()
        return copy

    owner_copy = load(owner_hbm, owner_ref, chunks + 2)
    local_copy = load(local_hbm, local_ref, chunks + 3)
    inc_copy = load(inc_hbm, inc, chunks)
    loads = []
    for t in range(chunks):
        part = pl.ds(t * per, per)
        loads.append(load(interp_hbm.at[part], interp.at[part], t))
    modes_copy = load(modes_hbm, modes_ref, chunks + 4)

    def member_at(k):
        third = lax.rem(k, 3)
        step = jnp.where(third == 0, 2, jnp.where(third == 1, 1, 3))
        step = jnp.where(k == n_member - 2, 0, step)
        core = lax.rem(group, 2)
        flip = (k < 3) | (k == n_member - 2)
        return lax.rem(group // 2 + step, n_member // 2) * 2 + jnp.where(flip, 1 - core, core)

    last = n_space - 1
    n_z = n_space // n_y
    my_z, my_y = me // n_y, lax.rem(me, n_y)

    def peer_at(p):
        k = last - p
        k_y, k_z = k // n_z, lax.rem(k, n_z)
        half = (k_z + 1) // 2
        up = lax.rem(k_z, 2) == 1
        step_z = jnp.where(up, half, n_z - half)
        device = lax.rem(my_z + step_z, n_z) * n_y + lax.rem(my_y + k_y, n_y)
        paired = (k_z == 0) | (k_z == n_z - 1)
        back_z = jnp.where(paired, k_z, jnp.where(up, k_z + 1, k_z - 1))
        return device, last - (lax.rem(n_y - k_y, n_y) * n_z + back_z)

    def position_of(device):
        step_z = (device // n_y - my_z + n_z) % n_z
        step_y = (device % n_y - my_y + n_y) % n_y
        k_z = jnp.where(
            step_z <= n_z // 2, jnp.maximum(2 * step_z - 1, 0), 2 * (n_z - step_z)
        )
        return last - (step_y * n_z + k_z)

    owner_copy.wait()
    local_copy.wait()
    owner_row = position_of(owner_ref[...]).astype(F32)
    down, across = iota((fine_count, fine_count), 0), iota((fine_count, fine_count), 1)
    owner_col = jnp.sum(jnp.where(down == across, owner_row, 0.0), axis=1, keepdims=True)
    same = owner_col == owner_row
    rank_row = jnp.sum(jnp.where(same & (down < across), 1.0, 0.0), axis=0, keepdims=True)
    rank_col = jnp.sum(jnp.where(same & (across < down), 1.0, 0.0), axis=1, keepdims=True)
    slot_row = owner_row * CAP + rank_row
    slot_col = owner_col * CAP + rank_col

    local_row = local_ref[...].astype(F32) + 1.0
    by_owner = jnp.where(
        iota((n_space, fine_count), 0).astype(F32) == owner_row, local_row, 0.0
    ).astype(BF16)
    by_rank = one_hot(iota((fine_count, 128), 1).astype(F32) == rank_col)
    table = dot(by_owner, by_rank)
    for d in range(n_space):
        idx_send[d] = table[d : d + 1, :]

    widen = one_hot(iota((fine_count, fine_rows), 1) // near == iota((fine_count, fine_rows), 0))
    place_row = dot(jnp.broadcast_to(slot_row, (8, fine_count)).astype(BF16), widen)[0:1]
    place_row = place_row * near + (iota((1, fine_rows), 1) % near).astype(F32)

    per_step = 8
    step_rows = per_step * rows
    for k in range(n_space // per_step):
        row = (iota((step_rows, fine_rows), 0) + k * step_rows).astype(F32)
        placing[k * step_rows : (k + 1) * step_rows, :] = one_hot(row == place_row)

    low = iota((4 * near, width), 1) < wide

    def turned(x):
        return pltpu.roll(x, wide, 1)

    inc_copy.wait()
    for t in range(chunks):
        loads[t].wait()

        @pl.loop(0, per // 4, unroll=2)
        def _(i):
            b = t * per + i * 4
            four = [dot(inc[b + q], interp[b + q]) for q in range(4)]
            first = jnp.concatenate([v[:near] for v in four], axis=0)
            second = jnp.concatenate([v[near:] for v in four], axis=0)
            at = pl.ds(pl.multiple_of(b * near, 4 * near), 4 * near)
            pieces[0, at, :] = jnp.where(low, first, turned(second)).astype(BF16)
            pieces[1, at, :] = jnp.where(low, turned(first), second).astype(BF16)

    ens_copy = load(ens_hbm, ens, chunks + 1)
    pl.semaphore_wait(barrier, n_space - 1 + n_member - 1)

    def space_copy(src, dst, d, phase):
        return pltpu.make_async_remote_copy(
            src_ref=src,
            dst_ref=dst,
            send_sem=send_sem.at[phase],
            recv_sem=recv_sem.at[phase],
            device_id={"space": d},
            device_id_type=MESH,
        )

    def member_copy(src, dst, d, phase):
        return pltpu.make_async_remote_copy(
            src_ref=src,
            dst_ref=dst,
            send_sem=send_sem.at[phase],
            recv_sem=recv_sem.at[phase],
            device_id={"member": d},
            device_id_type=MESH,
        )

    def send_idx(k, carry):
        d, there = peer_at(k)
        space_copy(idx_send.at[k], idx_recv.at[there], d, 0).start()
        return carry

    lax.fori_loop(0, last, send_idx, 0)

    for h in range(2):
        packed = pieces[h]

        def place(k, carry):
            at = pl.multiple_of(k * step_rows, step_rows)
            values = dot(placing[pl.ds(at, step_rows), :], packed)
            for q in range(per_step):
                p = k * per_step + q
                send[h, p] = values[q * rows : (q + 1) * rows, :].astype(BF16)

                @pl.when(p != last)
                def _():
                    d, there = peer_at(p)
                    space_copy(send.at[h, p], recv.at[h, there], d, 1 + h).start()

            return carry

        lax.fori_loop(0, n_space // per_step, place, 0)
        recv[h, last] = send[h, last]
    idx_recv[last] = idx_send[last]

    idx_all = space_copy(
        idx_send.at[pl.ds(0, n_space - 1)],
        idx_recv.at[pl.ds(0, n_space - 1)],
        lax.rem(me + 1, n_space),
        0,
    )
    idx_all.wait_recv()
    index = jnp.concatenate([idx_recv[s] for s in range(n_space)], axis=0).astype(BF16)
    lane_rank = one_hot((iota((128, slots), 1) % rows) // near == iota((128, slots), 0))
    by_source = dot(index, lane_rank)
    mine = iota((n_space, slots), 1) // rows == iota((n_space, slots), 0)
    index_row = jnp.sum(jnp.where(mine, by_source, 0.0), axis=0, keepdims=True)
    index_row = (index_row - 1.0) * near + (iota((1, slots), 1) % near).astype(F32)
    collect[...] = one_hot(iota((coarse_rows, slots), 0).astype(F32) == index_row)
    source_of = one_hot(iota((slots, n_space), 0) // rows == iota((slots, n_space), 1))
    by_row = dot(source_of, index)
    rank_of = (iota((slots, 128), 0) % rows) // near == iota((slots, 128), 1)
    index_col = jnp.sum(jnp.where(rank_of, by_row, 0.0), axis=1, keepdims=True)
    index_col = (index_col - 1.0) * near + (iota((slots, 1), 0) % near).astype(F32)
    spread[...] = one_hot(iota((slots, coarse_rows), 1).astype(F32) == index_col)

    modes_copy.wait()
    mix = lax.dot_general(
        modes_ref[...],
        modes_ref[...],
        (((0,), (0,)), ((), ())),
        precision=lax.Precision.HIGHEST,
        preferred_element_type=F32,
    )
    mix_high = mix.astype(BF16)
    mix_low = (mix - mix_high.astype(F32)).astype(BF16)
    mix_both = jnp.concatenate([mix_high, mix_low], axis=1)

    ens_copy.wait()
    half = iota((n_member * lev, width), 1) < wide

    @pl.loop(0, coarse)
    def _(c):
        for m in range(members // 2):
            one, two = ens[2 * m, c].astype(F32), ens[2 * m + 1, c].astype(F32)
            pairs[0, m, c] = jnp.where(half, one, turned(two)).astype(BF16)
            pairs[1, m, c] = jnp.where(half, turned(one), two).astype(BF16)

    others = pl.ds(0, n_member - 1)
    most = pl.ds(0, n_space - 1)
    next_member = lax.rem(group + 1, n_member)
    next_space = lax.rem(me + 1, n_space)
    part_rows = coarse_rows // parts

    def flat(messages):
        return messages.astype(F32).reshape(slots, width).astype(BF16)

    for h in range(2):
        space_copy(send.at[h, most], recv.at[h, most], next_space, 1 + h).wait_recv()
        restricted = dot(collect[...], flat(recv[h])).astype(BF16)
        for q in range(parts):
            levels_buf[h, q, group] = restricted[q * part_rows : (q + 1) * part_rows]

            def send_levels(k, carry):
                own = levels_buf.at[h, q, group]
                member_copy(own, own, member_at(k), 3 + h * parts + q).start()
                return carry

            lax.fori_loop(0, n_member - 1, send_levels, 0)

    @pl.loop(0, fine_count, unroll=4)
    def _(b):
        interp[b] = interp[b].T

    widen_col = one_hot(iota((fine_rows, fine_count), 0) // near == iota((fine_rows, fine_count), 1))
    slot_wide = jnp.broadcast_to(slot_col, (fine_count, 128)).astype(BF16)
    place_col = dot(widen_col, slot_wide) * near + (iota((fine_rows, 128), 0) % near).astype(F32)
    for t in range(slots // 128):
        unplace[:, t * 128 : (t + 1) * 128] = one_hot(
            place_col == (iota((fine_rows, 128), 1) + t * 128).astype(F32)
        )


    for h in range(2):
        for q in range(parts):
            theirs = levels_buf.at[h, q, others]
            member_copy(theirs, theirs, next_member, 3 + h * parts + q).wait_recv()

            def coarse_four(i, carry):
                at = pl.ds(pl.multiple_of(i * 4 * near, 4 * near), 4 * near)
                slabs = [levels_buf[h, q, g, at, :].astype(F32) for g in range(n_member)]
                other = [turned(slab) for slab in slabs]
                near_half = [jnp.where(low, x, y) for x, y in zip(slabs, other)]
                far_half = [jnp.where(low, y, x) for x, y in zip(slabs, other)]
                totals = []
                for e in range(4):
                    c = q * (coarse // parts) + i * 4 + e
                    cut = slice(e * near, (e + 1) * near)
                    here = jnp.concatenate(
                        [x[cut] for both in zip(near_half, far_half) for x in both], axis=0
                    ).astype(BF16)
                    schur = jnp.concatenate(
                        [pairs[h, m, c] * here for m in range(members // 2)], axis=1
                    )
                    rebuilt = dot(mix_both, jnp.concatenate([schur, schur], axis=0))
                    total = jnp.zeros(here.shape, F32)
                    for m in range(members // 2):
                        part = rebuilt[:, m * width : (m + 1) * width]
                        total += pairs[h, m, c].astype(F32) * part
                    totals.append(total + turned(total))
                for g in range(n_member):
                    top = [t[g * lev : g * lev + near] for t in totals]
                    end = [t[g * lev + near : (g + 1) * lev] for t in totals]
                    contrib[h, q, g, at, :] = jnp.where(
                        low, jnp.concatenate(top, axis=0), jnp.concatenate(end, axis=0)
                    ).astype(BF16)
                return carry

            lax.fori_loop(0, coarse // parts // 4, coarse_four, 0)

            def send_contrib(k, carry):
                d = member_at(k)
                member_copy(
                    contrib.at[h, q, d], arrived.at[h, q, group], d, 3 + (2 + h) * parts + q
                ).start()
                return carry

            lax.fori_loop(0, n_member - 1, send_contrib, 0)
            arrived[h, q, group] = contrib[h, q, group]

    for h in range(2):
        summed = []
        for q in range(parts):
            member_copy(
                contrib.at[h, q, others],
                arrived.at[h, q, others],
                next_member,
                3 + (2 + h) * parts + q,
            ).wait_recv()
            total = arrived[h, q, 0].astype(F32)
            for g in range(1, n_member):
                total += arrived[h, q, g].astype(F32)
            summed.append((total / scale).astype(BF16))
        applied = jnp.concatenate(summed, axis=0)

        def answer(k, carry):
            at = pl.multiple_of(k * step_rows, step_rows)
            values = dot(spread[pl.ds(at, step_rows), :], applied)
            for q in range(per_step):
                p = k * per_step + q
                reply[h, p] = values[q * rows : (q + 1) * rows, :].astype(BF16)

                @pl.when(p != last)
                def _():
                    d, there = peer_at(p)
                    space_copy(
                        reply.at[h, p], back.at[h, there], d, 3 + 4 * parts + h
                    ).start()

            return carry

        lax.fori_loop(0, n_space // per_step, answer, 0)
        back[h, last] = reply[h, last]

    for h in range(2):
        space_copy(
            reply.at[h, most], back.at[h, most], next_space, 3 + 4 * parts + h
        ).wait_recv()
        fine[h] = dot(unplace[...], flat(back[h]))
    first, second = fine[0], fine[1]
    left = iota((fine_rows, width), 1) < wide
    fine[0] = jnp.where(left, first, turned(second))
    fine[1] = jnp.where(left, turned(first), second)

    @pl.loop(0, fine_count // 2, unroll=4)
    def _(i):
        at = pl.ds(pl.multiple_of(i * 2 * near, 2 * near), 2 * near)
        top, end = fine[0, at, :], fine[1, at, :]
        for e in range(2):
            cut = slice(e * near, (e + 1) * near)
            values = jnp.concatenate([top[cut], end[cut]], axis=0).astype(BF16)
            out_ref[i * 2 + e] = dot(values, interp[i * 2 + e])

    def sent(src, d, make, phase):
        make(src, src, d, phase).wait_send()

    sent(idx_send.at[most], next_space, space_copy, 0)
    for h in range(2):
        sent(send.at[h, most], next_space, space_copy, 1 + h)
        for q in range(parts):
            sent(levels_buf.at[h, q, others], next_member, member_copy, 3 + h * parts + q)
            sent(contrib.at[h, q, others], next_member, member_copy, 3 + (2 + h) * parts + q)
        sent(reply.at[h, most], next_space, space_copy, 3 + 4 * parts + h)


def on_device(increment, interp, owner, local_block, ensemble, modes):
    fine_count, lev, width = increment.shape
    members, coarse, all_lev, _ = ensemble.shape
    n_space, n_member = lax.axis_size("space"), lax.axis_size("member")
    chunks = 6
    scale = float(members * n_member - 1)
    parts, n_y = 1, 4
    dims = (
        n_space, n_member, fine_count, lev, members, coarse, width, chunks, parts, n_y, scale
    )
    near = lev // 2
    rows = CAP * near
    slots = n_space * rows
    arguments = (
        interp,
        increment,
        ensemble,
        owner.reshape(1, fine_count),
        local_block.reshape(1, fine_count),
        modes.T,
    )
    hbm = pl.BlockSpec(memory_space=pltpu.HBM)
    vmem = pl.BlockSpec(memory_space=pltpu.VMEM)
    exchange = pltpu.VMEM((2, n_space, rows, width), BF16)
    by_group = pltpu.VMEM((2, parts, n_member, coarse // parts * near, width), BF16)
    return pl.pallas_call(
        functools.partial(kernel, dims),
        out_shape=jax.ShapeDtypeStruct((fine_count, lev, width), F32),
        in_specs=[hbm] * 6,
        out_specs=vmem,
        scratch_shapes=[
            pltpu.VMEM((1, fine_count), jnp.int32),
            pltpu.VMEM((1, fine_count), jnp.int32),
            pltpu.VMEM(modes.shape[::-1], F32),
            pltpu.VMEM(interp.shape, BF16),
            pltpu.VMEM(increment.shape, BF16),
            pltpu.VMEM(ensemble.shape, BF16),
            pltpu.VMEM((2, members // 2, *ensemble.shape[1:]), BF16),
            pltpu.VMEM((2, fine_count * near, width), BF16),
            exchange,
            exchange,
            pltpu.VMEM((n_space, 1, 128), F32),
            pltpu.VMEM((n_space, 1, 128), F32),
            pltpu.VMEM((slots, fine_count * near), BF16),
            pltpu.VMEM((fine_count * near, slots), BF16),
            pltpu.VMEM((coarse * near, slots), BF16),
            pltpu.VMEM((slots, coarse * near), BF16),
            by_group,
            by_group,
            by_group,
            exchange,
            exchange,
            pltpu.VMEM((2, fine_count * near, width), F32),
            pltpu.SemaphoreType.DMA((chunks + 5,)),
            pltpu.SemaphoreType.DMA((5 + 4 * parts,)),
            pltpu.SemaphoreType.DMA((5 + 4 * parts,)),
        ],
        compiler_params=pltpu.CompilerParams(
            collective_id=0, has_side_effects=True, vmem_limit_bytes=48 * 1024 * 1024
        ),
        name="covariance_apply",
    )(*[pltpu.with_memory_space_constraint(a, pltpu.HBM) for a in arguments])


def solution(mesh):
    in_specs = (
        P("space", "member", None),
        P("space", None, None),
        P("space", None),
        P("space"),
        P("member", "space", None, None),
        P(),
    )
    out_specs = P("space", "member", None)
    return jax.shard_map(
        on_device, mesh=mesh, in_specs=in_specs, out_specs=out_specs, check_vma=False
    )
```

time: 48.9 us -> 47.7 us (0.975)
  Pallas kernels: 48 us -> 46.7 us
    pallas_call x1, Pallas kernels: 48 us -> 46.7 us  [on_device(): pl.pallas_call(functools.partial(kernel, dims), out_shape=jax.ShapeDtypeS...]
where the time goes in v4:
time: 47.7 us; the launch traced here: 47.5 us
  Pallas kernels  46.7 us (98%)
  local copies, waits for them, and re-layouts  0.75 us (2%)
    pallas_call x1, Pallas kernels, on_device(): pl.pallas_call(functools.partial(kernel, dims), out_shape=jax.ShapeDtypeS...  46.7 us

profile of v4, /device:TPU:1, one launch (start us, length us, event | category | flops | bytes accessed | tf_op | source)
XLA Modules:
  0.0 47.5 jit_solution(6225940136183874969)
XLA Ops:
  0.0 46.7 %covariance_apply.1 = f32[96,8,128]{2,1,0:T(8,128)S(1)} custom-call(bf16[96,128,128]{2,1,0:T(8,128)(2,1)} %interp_hbm.1, bf16[96,8,128]{2,1,0:T(8,128)(2,1)} %inc_hbm.1, bf16[10,24,64,128]{3,2,1,0:T(8,128)(2,1)} %ens_hbm.1, s32[1,96]{1,0:T(1,128)} %bitcast.4, s32[1,96]{1,0:T(1,128)} %bitcast.5, f32[4,64]{1,0:T(4,128)} %bitcast.3), custom_call_target="tpu_custom_call" | custom-call | tf_op jit(solution)/shard_map/covariance_apply/pallas_call | solution.py:448
  46.7 0.7 %copy.8 = f32[96,8,128]{2,1,0:T(8,128)} copy(f32[96,8,128]{2,1,0:T(8,128)S(1)} %covariance_apply.1) | data formatting | bytes 786432

commit v5 on v4

--- a/solution.py
+++ b/solution.py
@@ -263,16 +263,21 @@
     mix_low = (mix - mix_high.astype(F32)).astype(BF16)
     mix_both = jnp.concatenate([mix_high, mix_low], axis=1)
 
+    half = iota((n_member * lev, width), 1) < wide
+
+    def pair_members(h):
+        @pl.loop(0, coarse)
+        def _(c):
+            for m in range(members // 2):
+                one, two = ens[2 * m, c], ens[2 * m + 1, c]
+                if h == 0:
+                    two = turned(two)
+                else:
+                    one = turned(one)
+                pairs[h, m, c] = jnp.where(half, one, two)
+
     ens_copy.wait()
-    half = iota((n_member * lev, width), 1) < wide
-
-    @pl.loop(0, coarse)
-    def _(c):
-        for m in range(members // 2):
-            one, two = ens[2 * m, c].astype(F32), ens[2 * m + 1, c].astype(F32)
-            pairs[0, m, c] = jnp.where(half, one, turned(two)).astype(BF16)
-            pairs[1, m, c] = jnp.where(half, turned(one), two).astype(BF16)
-
+    pair_members(0)
     others = pl.ds(0, n_member - 1)
     most = pl.ds(0, n_space - 1)
     next_member = lax.rem(group + 1, n_member)
@@ -295,18 +300,8 @@
 
             lax.fori_loop(0, n_member - 1, send_levels, 0)
 
-    @pl.loop(0, fine_count, unroll=4)
-    def _(b):
-        interp[b] = interp[b].T
-
-    widen_col = one_hot(iota((fine_rows, fine_count), 0) // near == iota((fine_rows, fine_count), 1))
-    slot_wide = jnp.broadcast_to(slot_col, (fine_count, 128)).astype(BF16)
-    place_col = dot(widen_col, slot_wide) * near + (iota((fine_rows, 128), 0) % near).astype(F32)
-    for t in range(slots // 128):
-        unplace[:, t * 128 : (t + 1) * 128] = one_hot(
-            place_col == (iota((fine_rows, 128), 1) + t * 128).astype(F32)
-        )
-
+        if h == 0:
+            pair_members(1)
 
     for h in range(2):
         for q in range(parts):
@@ -388,6 +383,19 @@
 
         lax.fori_loop(0, n_space // per_step, answer, 0)
         back[h, last] = reply[h, last]
+
+    @pl.loop(0, fine_count, unroll=4)
+    def _(b):
+        interp[b] = interp[b].T
+
+    widen_col = one_hot(iota((fine_rows, fine_count), 0) // near == iota((fine_rows, fine_count), 1))
+    slot_wide = jnp.broadcast_to(slot_col, (fine_count, 128)).astype(BF16)
+    place_col = dot(widen_col, slot_wide) * near + (iota((fine_rows, 128), 0) % near).astype(F32)
+    for t in range(slots // 128):
+        unplace[:, t * 128 : (t + 1) * 128] = one_hot(
+            place_col == (iota((fine_rows, 128), 1) + t * 128).astype(F32)
+        )
+
 
     for h in range(2):
         space_copy(

time: 47.7 us -> 45.5 us (0.954)
  Pallas kernels: 46.7 us -> 44.7 us
    pallas_call x1, Pallas kernels: 46.7 us -> 44.7 us  [on_device(): pl.pallas_call(functools.partial(kernel, dims), out_shape=jax.ShapeDtypeS...]
where the time goes in v5:
time: 45.5 us; the launch traced here: 45.4 us
  Pallas kernels  44.7 us (98%)
  local copies, waits for them, and re-layouts  0.75 us (2%)
    pallas_call x1, Pallas kernels, on_device(): pl.pallas_call(functools.partial(kernel, dims), out_shape=jax.ShapeDtypeS...  44.7 us

profile of v5, /device:TPU:1, one launch (start us, length us, event | category | flops | bytes accessed | tf_op | source)
XLA Modules:
  0.0 45.4 jit_solution(15684817151599894073)
XLA Ops:
  0.0 44.7 %covariance_apply.1 = f32[96,8,128]{2,1,0:T(8,128)S(1)} custom-call(bf16[96,128,128]{2,1,0:T(8,128)(2,1)} %interp_hbm.1, bf16[96,8,128]{2,1,0:T(8,128)(2,1)} %inc_hbm.1, bf16[10,24,64,128]{3,2,1,0:T(8,128)(2,1)} %ens_hbm.1, s32[1,96]{1,0:T(1,128)} %bitcast.4, s32[1,96]{1,0:T(1,128)} %bitcast.5, f32[4,64]{1,0:T(4,128)} %bitcast.3), custom_call_target="tpu_custom_call" | custom-call | tf_op jit(solution)/shard_map/covariance_apply/pallas_call | solution.py:456
  44.7 0.7 %copy.8 = f32[96,8,128]{2,1,0:T(8,128)} copy(f32[96,8,128]{2,1,0:T(8,128)S(1)} %covariance_apply.1) | data formatting | bytes 786432

commit v6 on v5

--- a/solution.py
+++ b/solution.py
@@ -169,7 +169,7 @@
     for t in range(chunks):
         loads[t].wait()
 
-        @pl.loop(0, per // 4, unroll=2)
+        @pl.loop(0, per // 4, unroll=4)
         def _(i):
             b = t * per + i * 4
             four = [dot(inc[b + q], interp[b + q]) for q in range(4)]
@@ -244,13 +244,6 @@
     index_row = jnp.sum(jnp.where(mine, by_source, 0.0), axis=0, keepdims=True)
     index_row = (index_row - 1.0) * near + (iota((1, slots), 1) % near).astype(F32)
     collect[...] = one_hot(iota((coarse_rows, slots), 0).astype(F32) == index_row)
-    source_of = one_hot(iota((slots, n_space), 0) // rows == iota((slots, n_space), 1))
-    by_row = dot(source_of, index)
-    rank_of = (iota((slots, 128), 0) % rows) // near == iota((slots, 128), 1)
-    index_col = jnp.sum(jnp.where(rank_of, by_row, 0.0), axis=1, keepdims=True)
-    index_col = (index_col - 1.0) * near + (iota((slots, 1), 0) % near).astype(F32)
-    spread[...] = one_hot(iota((slots, coarse_rows), 1).astype(F32) == index_col)
-
     modes_copy.wait()
     mix = lax.dot_general(
         modes_ref[...],
@@ -266,7 +259,7 @@
     half = iota((n_member * lev, width), 1) < wide
 
     def pair_members(h):
-        @pl.loop(0, coarse)
+        @pl.loop(0, coarse, unroll=4)
         def _(c):
             for m in range(members // 2):
                 one, two = ens[2 * m, c], ens[2 * m + 1, c]
@@ -350,6 +343,15 @@
             lax.fori_loop(0, n_member - 1, send_contrib, 0)
             arrived[h, q, group] = contrib[h, q, group]
 
+        if h == 0:
+            source_of = one_hot(iota((slots, n_space), 0) // rows == iota((slots, n_space), 1))
+            by_row = dot(source_of, index)
+            rank_of = (iota((slots, 128), 0) % rows) // near == iota((slots, 128), 1)
+            index_col = jnp.sum(jnp.where(rank_of, by_row, 0.0), axis=1, keepdims=True)
+            index_col = (index_col - 1.0) * near + (iota((slots, 1), 0) % near).astype(F32)
+            spread[...] = one_hot(iota((slots, coarse_rows), 1).astype(F32) == index_col)
+
+
     for h in range(2):
         summed = []
         for q in range(parts):
@@ -407,7 +409,7 @@
     fine[0] = jnp.where(left, first, turned(second))
     fine[1] = jnp.where(left, turned(first), second)
 
-    @pl.loop(0, fine_count // 2, unroll=4)
+    @pl.loop(0, fine_count // 2, unroll=12)
     def _(i):
         at = pl.ds(pl.multiple_of(i * 2 * near, 2 * near), 2 * near)
         top, end = fine[0, at, :], fine[1, at, :]

time: 45.5 us -> 44.5 us (0.978)
  Pallas kernels: 44.7 us -> 43.7 us
    pallas_call x1, Pallas kernels: 44.7 us -> 43.7 us  [on_device(): pl.pallas_call(functools.partial(kernel, dims), out_shape=jax.ShapeDtypeS...]
where the time goes in v6:
time: 44.5 us; the launch traced here: 44.4 us
  Pallas kernels  43.7 us (98%)
  local copies, waits for them, and re-layouts  0.75 us (2%)
    pallas_call x1, Pallas kernels, on_device(): pl.pallas_call(functools.partial(kernel, dims), out_shape=jax.ShapeDtypeS...  43.7 us

profile of v6, /device:TPU:1, one launch (start us, length us, event | category | flops | bytes accessed | tf_op | source)
XLA Modules:
  0.0 44.4 jit_solution(7222382884540629095)
XLA Ops:
  0.0 43.7 %covariance_apply.1 = f32[96,8,128]{2,1,0:T(8,128)S(1)} custom-call(bf16[96,128,128]{2,1,0:T(8,128)(2,1)} %interp_hbm.1, bf16[96,8,128]{2,1,0:T(8,128)(2,1)} %inc_hbm.1, bf16[10,24,64,128]{3,2,1,0:T(8,128)(2,1)} %ens_hbm.1, s32[1,96]{1,0:T(1,128)} %bitcast.4, s32[1,96]{1,0:T(1,128)} %bitcast.5, f32[4,64]{1,0:T(4,128)} %bitcast.3), custom_call_target="tpu_custom_call" | custom-call | tf_op jit(solution)/shard_map/covariance_apply/pallas_call | solution.py:458
  43.7 0.7 %copy.8 = f32[96,8,128]{2,1,0:T(8,128)} copy(f32[96,8,128]{2,1,0:T(8,128)S(1)} %covariance_apply.1) | data formatting | bytes 786432
